TPU v7x, 512 devices: a whole 4x8x8 slice. The times are simulated.
512 devices in a mesh: rows: 128 (over z, y, core), cols: 4 (over x).
Axes of the slice: x: 4, y: 8, z: 8, core: 2. Of those that a mesh axis runs over, the one named last changes fastest.
Arguments:
- hidden_panel: float32 [8192, 16384], P('cols', 'rows'), may hold values from -6 to 6
- row_signs: float32 [16384], P('rows'), may hold values from -1 to 1, as said below
- sample_rows: int32 [128, 4], P('rows'), may hold values from 0 to 16383, as said below
- sample_counts: int32 [128], replicated, may hold values from 1 to 4, as said below
- ridge_weight: float32 [], replicated, may hold values from 0.5 to 2
Outputs:
- sketch_gram: float32 [8192, 8192], P('cols', 'rows')
Inputs may be any that keep to these rules, and one draw needn't show every extreme that they name: `sample_rows`: row p holds 4 distinct row numbers of p * 128 to (p + 1) * 128 - 1 in ascending order, so the whole array ascends; only the first sample_counts[p] of them are sampled, the rest are ignored. `sample_counts`: entry p counts the live slots of block p; some block has exactly 4. `row_signs`: every entry is +1 or -1.
All inputs are finite; a program needn't handle non-finite values.
Results may differ from a plain program's by a relative error of at most 0.00008.
Values sent between devices are 32-bit elements; how exact they have to be, the bound alone decides.
A program may use at most 64 MiB of HBM per device.

v0:
```python
import math

import jax
import jax.numpy as jnp
from jax import lax
from jax.sharding import PartitionSpec as P


def swapped(value, axis, bit):
    mask = 2**bit
    pairs = [(source, source ^ mask) for source in range(lax.axis_size(axis))]
    return lax.ppermute(value, axis, pairs)


def parity_signs(common, levels):
    parity = jnp.zeros_like(common)
    for bit_level in range(levels):
        parity = parity ^ common >> bit_level & 1
    return (1 - 2 * parity).astype(jnp.float32)


def sign_table(extent):
    positions = jnp.arange(extent, dtype=jnp.int32)
    return parity_signs(positions[:, None] & positions[None, :], extent.bit_length() - 1)


def local_transform(signed):
    width, length = signed.shape
    outer_size = min(128, length)
    inner_size = length // outer_size
    blocks = signed.reshape(width, outer_size, inner_size)
    blocks = jnp.einsum(
        "cab,ea->ceb", blocks, sign_table(outer_size), precision=lax.Precision.HIGHEST
    )
    blocks = jnp.einsum(
        "ceb,fb->cef", blocks, sign_table(inner_size), precision=lax.Precision.HIGHEST
    )
    return blocks.reshape(width, length)


def body(hidden_panel, row_signs, sample_rows, sample_counts, ridge_weight):
    width, length = hidden_panel.shape
    shards = lax.axis_size("rows")
    my_shard = lax.axis_index("rows")
    levels = shards.bit_length() - 1
    factor = 1.0 / math.sqrt(length * shards)
    slot_total = sample_rows.shape[1]
    spread = local_transform(hidden_panel * row_signs[None, :])
    for bit_level in range(levels):
        partner = swapped(spread, "rows", bit_level)
        upper_half = my_shard >> bit_level & 1 == 1
        spread = jnp.where(upper_half, partner - spread, spread + partner)
    picked = jnp.take(spread, sample_rows[0] - my_shard * length, axis=1) * factor
    live_slots = lax.dynamic_index_in_dim(sample_counts, my_shard, keepdims=False)
    slot_mask = (jnp.arange(slot_total) < live_slots).astype(jnp.float32)
    sketch = picked * slot_mask[None, :]
    all_slots = lax.all_gather(sketch, "rows", axis=1, tiled=True)
    all_units = lax.all_gather(sketch, "cols", axis=0, tiled=True)
    block_units = lax.all_to_all(all_units, "rows", split_axis=0, concat_axis=1, tiled=True)
    partial_value = jnp.dot(
        all_slots,
        block_units.T,
        precision=lax.Precision.HIGHEST,
        preferred_element_type=jnp.float32,
    )
    sample_total = jnp.sum(sample_counts).astype(jnp.float32)
    row_start = lax.axis_index("cols") * width
    block_width = block_units.shape[0]
    col_start = my_shard * block_width
    diagonal = (
        (row_start + jnp.arange(width))[:, None] == (col_start + jnp.arange(block_width))[None, :]
    ).astype(jnp.float32)
    return partial_value / sample_total + ridge_weight * diagonal


def solution(mesh):
    placed = (P("cols", "rows"), P("rows"), P("rows", None), P(), P())
    return jax.shard_map(
        body, mesh=mesh, in_specs=placed, out_specs=P("cols", "rows"), check_vma=False
    )
```

profile of v0, /device:TPU:1, one launch (start us, length us, event | category | flops | bytes accessed | tf_op | source)
XLA Modules:
  0.0 380.0 jit_solution(14253344918159398699)
XLA Ops:
  6.5 2.3 convolution_bitcast_fusion
  8.8 8.8 %collective-permute-start = (f32[2048,128]{0,1:T(8,128)S(1)}, f32[2048,128]{0,1:T(8,128)S(1)}, u32[]{:S(2)}, u32[]{:S(2)}) collective-permute-start(f32[2048,128]{0,1:T(8,128)S(1)} %convolution_bitcast_fusion), channel_id=1, source_target_pairs={{0,4},{4,0},{8,12},{12,8},{16,20},{20,16},{24,28},{28,24},{32,36},... | collective-permute-start | bytes 3145736 | tf_op jit(solution)/shard_map/ppermute | solution.py:12
  17.6 2.3 collective-permute-done
  20.0 1.9 collective-permute-start.1
  22.0 24.3 %collective-permute-done.1 = f32[2048,128]{0,1:T(8,128)S(1)} collective-permute-done((f32[2048,128]{0,1:T(8,128)S(1)}, f32[2048,128]{0,1:T(8,128)S(1)}, u32[]{:S(2)}, u32[]{:S(2)}) %collective-permute-start.1) | collective-permute-done | bytes 1048608 | tf_op jit(solution)/shard_map/ppermute | solution.py:12
  46.5 1.9 collective-permute-start.2
  48.4 48.4 %collective-permute-done.2 = f32[2048,128]{0,1:T(8,128)S(1)} collective-permute-done((f32[2048,128]{0,1:T(8,128)S(1)}, f32[2048,128]{0,1:T(8,128)S(1)}, u32[]{:S(2)}, u32[]{:S(2)}) %collective-permute-start.2) | collective-permute-done | bytes 1048608 | tf_op jit(solution)/shard_map/ppermute | solution.py:12
  96.9 2.0 collective-permute-start.3
  99.0 47.9 %collective-permute-done.3 = f32[2048,128]{0,1:T(8,128)S(1)} collective-permute-done((f32[2048,128]{0,1:T(8,128)S(1)}, f32[2048,128]{0,1:T(8,128)S(1)}, u32[]{:S(2)}, u32[]{:S(2)}) %collective-permute-start.3) | collective-permute-done | bytes 1048608 | tf_op jit(solution)/shard_map/ppermute | solution.py:12
  147.0 1.9 collective-permute-start.4
  148.9 23.2 %collective-permute-done.4 = f32[2048,128]{0,1:T(8,128)S(1)} collective-permute-done((f32[2048,128]{0,1:T(8,128)S(1)}, f32[2048,128]{0,1:T(8,128)S(1)}, u32[]{:S(2)}, u32[]{:S(2)}) %collective-permute-start.4) | collective-permute-done | bytes 1048608 | tf_op jit(solution)/shard_map/ppermute | solution.py:12
  172.2 4.7 %collective-permute-start.5 = (f32[2048,128]{0,1:T(8,128)S(1)}, f32[2048,128]{0,1:T(8,128)S(1)}, u32[]{:S(2)}, u32[]{:S(2)}) collective-permute-start(f32[2048,128]{0,1:T(8,128)S(1)} %add_select_fusion.2), channel_id=1, source_target_pairs={{0,128},{4,132},{8,136},{12,140},{16,144},{20,148},{24,152},{28,15... | collective-permute-start | bytes 3145736 | tf_op jit(solution)/shard_map/ppermute | solution.py:12
  176.9 45.1 %collective-permute-done.5 = f32[2048,128]{0,1:T(8,128)S(1)} collective-permute-done((f32[2048,128]{0,1:T(8,128)S(1)}, f32[2048,128]{0,1:T(8,128)S(1)}, u32[]{:S(2)}, u32[]{:S(2)}) %collective-permute-start.5) | collective-permute-done | bytes 1048608 | tf_op jit(solution)/shard_map/ppermute | solution.py:12
  222.2 8.2 %collective-permute-start.6 = (f32[2048,128]{0,1:T(8,128)S(1)}, f32[2048,128]{0,1:T(8,128)S(1)}, u32[]{:S(2)}, u32[]{:S(2)}) collective-permute-start(f32[2048,128]{0,1:T(8,128)S(1)} %add_select_fusion.1), channel_id=1, source_target_pairs={{0,256},{4,260},{8,264},{12,268},{16,272},{20,276},{24,280},{28,28... | collective-permute-start | bytes 3145736 | tf_op jit(solution)/shard_map/ppermute | solution.py:12
  230.3 0.6 dynamic_slice.4
  230.9 0.6 compare_select_fusion.2
  231.6 43.6 %collective-permute-done.6 = f32[2048,128]{0,1:T(8,128)S(1)} collective-permute-done((f32[2048,128]{0,1:T(8,128)S(1)}, f32[2048,128]{0,1:T(8,128)S(1)}, u32[]{:S(2)}, u32[]{:S(2)}) %collective-permute-start.6) | collective-permute-done | bytes 1048608 | tf_op jit(solution)/shard_map/ppermute | solution.py:12
  275.4 0.6 gather_fusion
  275.9 0.7 fusion.37
  276.6 9.5 %all_gather.7 = f32[8192,4]{0,1:T(4,128)S(1)} all-gather(f32[2048,4]{0,1:T(4,128)S(1)} %get-tuple-element.5), channel_id=1, replica_groups=mesh['rows'=128,'cols'=4] {'cols'}, dimensions={0}, use_global_device_ids=true | all-gather | bytes 163840 | tf_op jit(solution)/shard_map/all_gather | solution.py:58
  286.1 0.2 all_to_all.14
  286.3 0.2 copy.9
  286.5 0.9 reshape.65
  287.4 15.0 %all-to-all-start = ((f32[128,1,256]{2,1,0:T(1,128)}), f32[128,1,256]{2,1,0:T(1,128)S(1)}, u32[]{:S(2)}, u32[]{:S(2)}) async-start(f32[128,1,256]{2,1,0:T(1,128)} %reshape.65), calls=%async_computation | async-start | bytes 262144 | tf_op jit(solution)/shard_map/all_to_all | solution.py:59
  302.4 0.6 reduce_sum.9
  304.3 11.1 %all-to-all-done = f32[128,1,256]{2,1,0:T(1,128)S(1)} async-done(((f32[128,1,256]{2,1,0:T(1,128)}), f32[128,1,256]{2,1,0:T(1,128)S(1)}, u32[]{:S(2)}, u32[]{:S(2)}) %all-to-all-start) | async-done | bytes 131104 | tf_op jit(solution)/shard_map/all_to_all | solution.py:59
  315.4 0.5 broadcast.102
  315.9 1.0 reduce
  316.9 0.2 reshape.66
  317.0 45.1 %all-gather.3.cloned.1.call-done = f32[128,4,2048]{2,1,0:T(4,128)} async-done(((f32[1,4,2048]{2,1,0:T(4,128)}), f32[128,4,2048]{2,1,0:T(4,128)}) %all-gather.3.cloned.1.call-update) | async-done | bytes 4194320 | tf_op jit(solution)/shard_map/all_gather | solution.py:57
  362.1 5.3 %reshape.64 = f32[512,2048]{1,0:T(8,128)} reshape(f32[128,4,2048]{2,1,0:T(4,128)} %all-gather.3.cloned.1.call-done) | data formatting | bytes 8388608
  367.4 5.8 %fusion = f32[2048,64]{0,1:T(8,128)} fusion(f32[512,2048]{1,0:T(8,128)} %reshape.64, f32[64,512]{0,1:T(8,128)S(1)} %bitcast.28, f32[]{:T(128)S(6)} %copy.10, s32[2048]{0:T(1024)S(1)} %iota_add_fusion, f32[]{:T(128)S(6)} %convert_element_type.13, s32[64]{0:T(128)S(1)} %iota_add_fusion.1), kind=kOutput, calls=%fused_computation.3 | convolution fusion | flops 805830656 | bytes 4858120 | tf_op jit(solution)/shard_map/dot_general | solution.py:60
  (18 shorter events, 1.1 us)
Async XLA Ops:
  6.5 355.6 %all-gather.3.cloned.1.call-start = ((), (), s32[]{:S(2)}) async-start(), calls=%async_computation.1 | async-start | bytes 4227072 | tf_op jit(solution)/shard_map/all_gather | solution.py:57
  8.8 11.1 %collective-permute-start = (f32[2048,128]{0,1:T(8,128)S(1)}, f32[2048,128]{0,1:T(8,128)S(1)}, u32[]{:S(2)}, u32[]{:S(2)}) collective-permute-start(f32[2048,128]{0,1:T(8,128)S(1)} %convolution_bitcast_fusion), channel_id=1, source_target_pairs={{0,4},{4,0},{8,12},{12,8},{16,20},{20,16},{24,28},{28,24},{32,36},... | collective-permute-start | bytes 3145736 | tf_op jit(solution)/shard_map/ppermute | solution.py:12
  20.0 26.3 %collective-permute-start.1 = (f32[2048,128]{0,1:T(8,128)S(1)}, f32[2048,128]{0,1:T(8,128)S(1)}, u32[]{:S(2)}, u32[]{:S(2)}) collective-permute-start(f32[2048,128]{0,1:T(8,128)S(1)} %add_select_fusion.6), channel_id=1, source_target_pairs={{0,8},{4,12},{8,0},{12,4},{16,24},{20,28},{24,16},{28,20},{32,40},... | collective-permute-start | bytes 3145736 | tf_op jit(solution)/shard_map/ppermute | solution.py:12
  46.5 50.3 %collective-permute-start.2 = (f32[2048,128]{0,1:T(8,128)S(1)}, f32[2048,128]{0,1:T(8,128)S(1)}, u32[]{:S(2)}, u32[]{:S(2)}) collective-permute-start(f32[2048,128]{0,1:T(8,128)S(1)} %add_select_fusion.5), channel_id=1, source_target_pairs={{0,16},{4,20},{8,24},{12,28},{16,0},{20,4},{24,8},{28,12},{32,48},... | collective-permute-start | bytes 3145736 | tf_op jit(solution)/shard_map/ppermute | solution.py:12
  96.9 49.9 %collective-permute-start.3 = (f32[2048,128]{0,1:T(8,128)S(1)}, f32[2048,128]{0,1:T(8,128)S(1)}, u32[]{:S(2)}, u32[]{:S(2)}) collective-permute-start(f32[2048,128]{0,1:T(8,128)S(1)} %add_select_fusion.4), channel_id=1, source_target_pairs={{0,32},{4,36},{8,40},{12,44},{16,48},{20,52},{24,56},{28,60},{32,0... | collective-permute-start | bytes 3145736 | tf_op jit(solution)/shard_map/ppermute | solution.py:12
  98.9 131.4 %copy-start.1 = (s32[128]{0:T(128)S(1)}, s32[128]{0:T(128)}, u32[]{:S(2)}) copy-start(s32[128]{0:T(128)} %param.8) | copy-start | bytes 1540
  98.9 132.7 %copy-start = (s32[1,4]{1,0:T(1,128)S(1)}, s32[1,4]{1,0:T(1,128)}, u32[]{:S(2)}) copy-start(s32[1,4]{1,0:T(1,128)} %param.7) | copy-start | bytes 52
  147.0 25.1 %collective-permute-start.4 = (f32[2048,128]{0,1:T(8,128)S(1)}, f32[2048,128]{0,1:T(8,128)S(1)}, u32[]{:S(2)}, u32[]{:S(2)}) collective-permute-start(f32[2048,128]{0,1:T(8,128)S(1)} %add_select_fusion.3), channel_id=1, source_target_pairs={{0,64},{4,68},{8,72},{12,76},{16,80},{20,84},{24,88},{28,92},{32,9... | collective-permute-start | bytes 3145736 | tf_op jit(solution)/shard_map/ppermute | solution.py:12
  172.2 49.8 %collective-permute-start.5 = (f32[2048,128]{0,1:T(8,128)S(1)}, f32[2048,128]{0,1:T(8,128)S(1)}, u32[]{:S(2)}, u32[]{:S(2)}) collective-permute-start(f32[2048,128]{0,1:T(8,128)S(1)} %add_select_fusion.2), channel_id=1, source_target_pairs={{0,128},{4,132},{8,136},{12,140},{16,144},{20,148},{24,152},{28,15... | collective-permute-start | bytes 3145736 | tf_op jit(solution)/shard_map/ppermute | solution.py:12
  222.2 53.0 %collective-permute-start.6 = (f32[2048,128]{0,1:T(8,128)S(1)}, f32[2048,128]{0,1:T(8,128)S(1)}, u32[]{:S(2)}, u32[]{:S(2)}) collective-permute-start(f32[2048,128]{0,1:T(8,128)S(1)} %add_select_fusion.1), channel_id=1, source_target_pairs={{0,256},{4,260},{8,264},{12,268},{16,272},{20,276},{24,280},{28,28... | collective-permute-start | bytes 3145736 | tf_op jit(solution)/shard_map/ppermute | solution.py:12
  287.4 28.0 %all-to-all-start = ((f32[128,1,256]{2,1,0:T(1,128)}), f32[128,1,256]{2,1,0:T(1,128)S(1)}, u32[]{:S(2)}, u32[]{:S(2)}) async-start(f32[128,1,256]{2,1,0:T(1,128)} %reshape.65), calls=%async_computation | async-start | bytes 262144 | tf_op jit(solution)/shard_map/all_to_all | solution.py:59
Sparse Core Ops, SparseCore 0:
  276.8 85.2 all-gather.2
where the time goes:
time: 381 us; the launch traced here: 380 us
  waiting for transfers between devices  291 us (76%)
  starting transfers between devices  44.5 us (12%)
  between operations  14.9 us (4%)
  blocking collectives  9.46 us (2%)
  local copies, waits for them, and re-layouts  8.41 us (2%)
  matrix products  8.04 us (2%)
  other arithmetic  3.98 us (1%)
    ppermute x7, waiting for transfers between devices, swapped(): return lax.ppermute(value, axis, pairs)  235 us
    all_gather x1, waiting for transfers between devices, body(): all_slots = lax.all_gather(sketch, 'rows', axis=1, tiled=True)  45.1 us
    ppermute x7, starting transfers between devices, swapped(): return lax.ppermute(value, axis, pairs)  29.4 us
    all_to_all x1, starting transfers between devices, body(): lax.all_to_all(all_units, 'rows', split_axis=0, concat_axis=1, tiled=True)  15 us
    all_to_all x1, waiting for transfers between devices, body(): lax.all_to_all(all_units, 'rows', split_axis=0, concat_axis=1, tiled=True)  11.1 us
    all_gather x1, blocking collectives, body(): all_units = lax.all_gather(sketch, 'cols', axis=0, tiled=True)  9.46 us
  transfers between devices with their start and end apart: 9, of which 9 were waited for; matrix products, arithmetic and copies ran while one was open for 1% of the time, Pallas kernels for 0%

commit v1 on v0

v1 whole, which is shorter than its diff:
```python
import functools
import math

import jax
import jax.numpy as jnp
from jax import lax
from jax.experimental import pallas as pl
from jax.experimental.pallas import tpu as pltpu
from jax.sharding import PartitionSpec as P

MESH = pl.DeviceIdType.MESH


def halves(value):
    high = value.astype(jnp.bfloat16)
    return high, (value - high.astype(jnp.float32)).astype(jnp.bfloat16)


def signs_of(common):
    for shift in (8, 4, 2, 1):
        common = common ^ (common >> shift)
    return (1 - 2 * (common & 1)).astype(jnp.float32)


def far_first(n):
    return [n // 2] + [d for k in range(n // 2 - 1, 0, -1) for d in (k, n - k)]


def kernel(
    nz, ny, nx, cap, panel, signs, rows, counts, ridge, out,
    xs, ra, rb, sm1, sm2, pa, pb, qa, qb, sa, sb, bo, b2, hh, ob, st,
    in_sem, out_sem, s_raw, r_raw, s_sm1, r_sm1, s_sm2, r_sm2, s_red, r_red, s_ag, r_ag,
    s_op, r_op, s_x, r_x, s_sib, r_sib, s_ring, r_ring, s_out, r_out,
):
    length = panel.shape[-1]
    shards = counts.shape[1]
    me = lax.axis_index("rows")
    q = lax.axis_index("cols")
    c = lax.rem(me, 2)
    y = lax.rem(me // 2, ny)
    z = me // (2 * ny)
    mate = 1 - c

    def at(zz, yy, cc, xx):
        return ((zz * ny + yy) * 2 + cc, xx)

    def up_z(d):
        return lax.rem(z + d, nz)

    def up_y(d):
        return lax.rem(y + d, ny)

    pending = []

    def send(src, dst, ss, rs, to, keep=True):
        copy = pltpu.make_async_remote_copy(
            src_ref=src, dst_ref=dst, send_sem=ss, recv_sem=rs, device_id=to, device_id_type=MESH
        )
        copy.start()
        if keep:
            pending.append(copy)
        return copy

    def arrived(slot, sem):
        pltpu.make_async_copy(slot, slot, sem).wait()

    load = pltpu.make_async_copy(panel, xs, in_sem)
    load.start()

    barrier = pltpu.get_barrier_semaphore()
    greeted = [at(z, y, mate, q)]
    for d in range(1, nz):
        greeted += [at(up_z(d), y, cc, q) for cc in (0, 1)]
    for d in range(1, ny):
        greeted += [at(z, up_y(d), cc, q) for cc in (0, 1)]
    for d in range(1, nx):
        greeted.append(at(z, y, c, lax.rem(q + d, nx)))
    for to in greeted:
        pl.semaphore_signal(barrier, inc=1, device_id=to, device_id_type=MESH)

    count_row = counts[...].astype(jnp.float32)
    lane = lax.broadcasted_iota(jnp.int32, (shards, shards), 1)
    line = lax.broadcasted_iota(jnp.int32, (shards, shards), 0)
    ends = jnp.sum(jnp.where(lane <= line, count_row, 0.0), axis=1, keepdims=True)
    slot = lax.broadcasted_iota(jnp.int32, (1, cap), 1)
    passed = ends <= slot.astype(jnp.float32)
    pk = jnp.sum(passed.astype(jnp.float32), axis=0, keepdims=True).astype(jnp.int32)
    block = lax.broadcasted_iota(jnp.int32, (1, shards), 1)
    before = jnp.sum(jnp.where(block < me, count_row, 0.0), axis=1, keepdims=True)
    total = jnp.sum(count_row, axis=1, keepdims=True)
    place = slot - before.astype(jnp.int32)
    own = jnp.zeros((1, cap), jnp.int32)
    for j in range(rows.shape[1]):
        own = jnp.where((pk == me) & (place == j), rows[0, j] - me * length, own)
    sm1[z, c] = own

    load.wait()
    xs[...] = xs[...] * signs[...]
    pl.semaphore_wait(barrier, len(greeted))

    send(sm1.at[z, c], sm1.at[z, c], s_sm1.at[0, 0], r_sm1.at[0, c], at(z, y, mate, q))
    for d in range(1, nz):
        for cc in (0, 1):
            send(sm1.at[z, c], sm1.at[z, c], s_sm1.at[d, cc], r_sm1.at[d, c], at(up_z(d), y, cc, q))

    def raw_z(d):
        for cc in (0, 1):
            send(xs.at[cc, :, 0, up_z(d)], ra.at[z, c], s_raw.at[0, d, cc], r_raw.at[0, d, c], at(up_z(d), y, cc, q))

    def raw_y(d):
        for cc in (0, 1):
            send(xs.at[cc, up_y(d), 1], rb.at[y, c], s_raw.at[1, d, cc], r_raw.at[1, d, c], at(z, up_y(d), cc, q))

    order_z, order_y = far_first(nz), far_first(ny)
    split = min(3, len(order_y))
    for k in range(max(len(order_z), split)):
        if k < len(order_z):
            raw_z(order_z[k])
        if k < split:
            raw_y(order_y[k])
    send(xs.at[mate, :, 0, z], ra.at[z, c], s_raw.at[0, 0, 0], r_raw.at[0, 0, c], at(z, y, mate, q))
    send(xs.at[mate, y, 1], rb.at[y, c], s_raw.at[1, 0, 0], r_raw.at[1, 0, c], at(z, y, mate, q))

    arrived(sm1.at[z, mate], r_sm1.at[0, mate])
    for d in range(1, nz):
        for cc in (0, 1):
            arrived(sm1.at[up_z(nz - d), cc], r_sm1.at[d, cc])
    sm2[y] = jnp.sum(sm1[...].reshape(2 * nz, 1, cap), axis=0)
    for d in range(1, ny):
        send(sm2.at[y], sm2.at[y], s_sm2.at[d], r_sm2.at[d], at(z, up_y(d), c, q))
    for d in order_y[split:]:
        raw_y(d)
    for d in range(1, ny):
        arrived(sm2.at[up_y(ny - d)], r_sm2.at[d])
    local_row = jnp.sum(sm2[...], axis=0)

    token = lax.broadcasted_iota(jnp.int32, (length, cap), 0)
    scale = 1.0 / math.sqrt(length * shards)
    live = jnp.where(slot.astype(jnp.float32) < total, scale, 0.0)
    sign = (signs_of(token & local_row) * live).astype(jnp.bfloat16)
    hh[:length] = sign
    hh[length:] = sign

    def share(parts, acc):
        pieces = [jnp.concatenate(halves(value), axis=1) for value, _ in parts]
        made = jnp.dot(jnp.concatenate(pieces, axis=0), hh[...], preferred_element_type=jnp.float32)
        high = made.shape[0] // len(parts)
        for k, (_, source) in enumerate(parts):
            term = made[k * high : (k + 1) * high] * signs_of(pk & source)
            acc = term if acc is None else acc + term
        return acc

    def batches(n):
        return [(0,)] + [(d, n - d) for d in range(1, n // 2)] + [(n // 2,)]

    def flat(value):
        return value.reshape(-1, value.shape[-1])

    def block_of(zz, yy, cc):
        return (zz * ny + yy) * 2 + cc

    def share_z():
        acc = None
        for batch in batches(nz):
            parts = []
            for d in batch:
                zz = up_z(nz - d) if d else z
                for cc in (0, 1):
                    if d == 0 and cc == 0:
                        parts.append((flat(xs[c, :, 0, z]), block_of(z, y, c)))
                        continue
                    source = mate if d == 0 else cc
                    arrived(ra.at[zz, source], r_raw.at[0, d, source])
                    parts.append((flat(ra[zz, source]), block_of(zz, y, source)))
            acc = share(parts, acc)
        return acc

    def share_y():
        acc = None
        for batch in batches(ny):
            parts = []
            for d in batch:
                yy = up_y(ny - d) if d else y
                for cc in (0, 1):
                    if d == 0 and cc == 0:
                        parts.append((flat(xs[c, y, 1]), block_of(z, y, c)))
                        continue
                    source = mate if d == 0 else cc
                    arrived(rb.at[yy, source], r_raw.at[1, d, source])
                    parts.append((flat(rb[yy, source]), block_of(z, yy, source)))
            acc = share(parts, acc)
        return acc

    pa[...] = share_z().reshape(ny, 8, cap)
    for d in far_first(ny):
        send(pa.at[up_y(d)], qa.at[y], s_red.at[0, d], r_red.at[0, d], at(z, up_y(d), c, q))
    pb[...] = share_y().reshape(nz, 8, cap)
    for d in far_first(nz):
        send(pb.at[up_z(d)], qb.at[z], s_red.at[1, d], r_red.at[1, d], at(up_z(d), y, c, q))

    piece = pa[y]
    for d in range(1, ny):
        arrived(qa.at[up_y(ny - d)], r_red.at[0, d])
        piece = piece + qa[up_y(ny - d)]
    sa[y, z] = piece
    for d in far_first(nz):
        send(sa.at[y, z], sa.at[y, z], s_ag.at[0, d], r_ag.at[0, d], at(up_z(d), y, c, q))
    piece = pb[z]
    for d in range(1, nz):
        arrived(qb.at[up_z(nz - d)], r_red.at[1, d])
        piece = piece + qb[up_z(nz - d)]
    sb[z, y] = piece
    for d in far_first(ny):
        send(sb.at[z, y], sb.at[z, y], s_ag.at[1, d], r_ag.at[1, d], at(z, up_y(d), c, q))

    target = 2 * q + c
    hop = lax.rem(target - z + nz, nz)

    @pl.when(hop != 0)
    def _():
        send(sb.at[z, y], bo.at[1, z], s_op.at[hop], r_op.at[hop], at(target, y, c, q), keep=False)

    @pl.when(hop == 0)
    def _():
        bo[1, z] = piece

    for d in range(1, nz):
        arrived(sa.at[y, up_z(nz - d)], r_ag.at[0, d])

    def ring(which, sign_of, d):
        n, mine, buf = (ny, y, sa) if which == 0 else (nz, z, sb)
        chunk = lax.rem(mine + n - d, n) if sign_of == 0 else lax.rem(mine + d, n)
        step = 1 if sign_of == 0 else n - 1
        there = lax.rem(mine + step, n)
        to = at(z, there, c, q) if which == 0 else at(there, y, c, q)
        view = buf.at[chunk]
        if d == n // 2 - 1:
            half = buf.shape[1] // 2
            view = buf.at[chunk, pl.ds(0 if sign_of == 0 else half, half)]
        send(view, view, s_ring.at[which, sign_of, d], r_ring.at[which, sign_of, d], to)

    def ring_wait(which, sign_of, d):
        n, mine, buf = (ny, y, sa) if which == 0 else (nz, z, sb)
        chunk = lax.rem(mine + n - d, n) if sign_of == 0 else lax.rem(mine + d, n)
        view = buf.at[chunk]
        if d == n // 2:
            half = buf.shape[1] // 2
            view = buf.at[chunk, pl.ds(0 if sign_of == 0 else half, half)]
        arrived(view, r_ring.at[which, sign_of, d - 1])

    for way in (0, 1):
        ring(0, way, 0)
    for d in range(1, ny):
        arrived(sb.at[z, up_y(ny - d)], r_ag.at[1, d])
    for way in (0, 1):
        ring(1, way, 0)

    root_c = lax.rem(z, 2)
    root_q = z // 2

    @pl.when((c == root_c) & (q == root_q))
    def _():
        for d in range(1, nz):
            arrived(bo.at[1, up_z(nz - d)], r_op.at[d])
        bo[0] = sa[y]
        for h in (0, 1):
            src = sa.at[y] if h == 0 else bo.at[1]
            for d in range(1, nx):
                send(src, bo.at[h], s_x.at[h, d], r_x.at[h, d], at(z, y, c, lax.rem(q + d, nx)), keep=False)
            send(src, bo.at[h], s_sib.at[h], r_sib.at[h], at(z, y, mate, q), keep=False)

    def ring_step(d):
        for which, n in ((0, ny), (1, nz)):
            if d < n // 2:
                for way in (0, 1):
                    ring_wait(which, way, d)
                    ring(which, way, d)

    top = max(ny, nz) // 2
    for d in range(1, top - 1):
        ring_step(d)

    away = lax.rem(q - root_q + nx, nx)

    @pl.when((c == root_c) & (q != root_q))
    def _():
        for h in (0, 1):
            arrived(bo.at[h], r_x.at[h, away])
            send(bo.at[h], bo.at[h], s_sib.at[h], r_sib.at[h], at(z, y, mate, q), keep=False)

    if top > 1:
        ring_step(top - 1)

    @pl.when(c != root_c)
    def _():
        for h in (0, 1):
            arrived(bo.at[h], r_sib.at[h])

    wide = 2 * nz * 8
    half_wide = wide // 2
    b_high, b_low = halves(flat(bo[...].reshape(2 * nz, 8, cap)))
    b2[:wide] = b_high
    b2[wide:] = b_low
    units = 2 * ny * wide
    first = q * units + c * (ny * wide)
    col = (z * ny + y) * wide + lax.broadcasted_iota(jnp.int32, (1, wide), 1)
    inverse = 1.0 / total
    weight = ridge[0, 0]

    def gram(which, chunk):
        value = flat(sa[chunk] if which == 0 else sb[chunk])
        high = value.shape[0]
        both = jnp.concatenate(halves(value), axis=0)
        made = lax.dot_general(both, b2[...], (((1,), (1,)), ((), ())), preferred_element_type=jnp.float32)
        made = made[:high] + made[high:]
        made = made[:, :wide] + made[:, wide:]
        r = lax.broadcasted_iota(jnp.int32, (high, 1), 0)
        if which == 0:
            unit = first + chunk * wide + r
        else:
            unit = first + (r // 8) * wide + half_wide + chunk * 8 + lax.rem(r, 8)
        made = made * inverse + jnp.where(unit == col, weight, 0.0)
        left, right = made[:, :half_wide], made[:, half_wide:]
        mine = jnp.where(c == 0, left, right).reshape(-1, 8, half_wide)
        theirs = jnp.where(c == 0, right, left).reshape(-1, 8, half_wide)
        return mine, theirs

    def emit(which, d):
        n, mine_at = (ny, y) if which == 0 else (nz, z)
        chunk = lax.rem(mine_at + d, n)
        mine, theirs = gram(which, chunk)
        if which == 0:
            ob[c, chunk, 0] = mine
            st[chunk, 0] = theirs
            src, dst = st.at[chunk, 0], ob.at[c, chunk, 0]
        else:
            ob[c, :, 1, chunk] = mine
            st[:, 1, chunk] = theirs
            src, dst = st.at[:, 1, chunk], ob.at[c, :, 1, chunk]
        send(src, dst, s_out.at[which, d], r_out.at[which, d], at(z, y, mate, q))

    for d in range(nz):
        if d != nz // 2:
            emit(1, d)
    for d in range(ny):
        if d != ny // 2:
            emit(0, d)
    for which, n in ((0, ny), (1, nz)):
        for way in (0, 1):
            ring_wait(which, way, n // 2)
        emit(which, n // 2)

    mine_out = pltpu.make_async_copy(ob.at[c], out.at[c], out_sem.at[0])
    mine_out.start()
    for which, n in ((0, ny), (1, nz)):
        for d in range(n):
            chunk = lax.rem((y if which == 0 else z) + d, n)
            arrived(ob.at[mate, chunk, 0] if which == 0 else ob.at[mate, :, 1, chunk], r_out.at[which, d])
    mate_out = pltpu.make_async_copy(ob.at[mate], out.at[mate], out_sem.at[1])
    mate_out.start()

    for copy in pending:
        copy.wait_send()

    def sent(src, sem):
        pltpu.make_async_copy(src, src, sem).wait()

    @pl.when(hop != 0)
    def _():
        sent(sb.at[z, y], s_op.at[hop])

    @pl.when((c == root_c) & (q == root_q))
    def _():
        for h in (0, 1):
            for d in range(1, nx):
                sent(bo.at[h], s_x.at[h, d])

    @pl.when(c == root_c)
    def _():
        for h in (0, 1):
            sent(bo.at[h], s_sib.at[h])

    mine_out.wait()
    mate_out.wait()


def body(hidden_panel, row_signs, sample_rows, sample_counts, ridge_weight):
    nx = lax.axis_size("cols")
    nz = 2 * nx
    ny = lax.axis_size("rows") // (2 * nz)
    width, length = hidden_panel.shape
    shards = sample_counts.shape[0]
    cap = -(-shards * sample_rows.shape[1] // 128) * 128
    half_wide = 8 * nz
    dma, f32, i32, bf16 = pltpu.SemaphoreType.DMA, jnp.float32, jnp.int32, jnp.bfloat16
    m = max(nz, ny)
    vmem = pl.BlockSpec(memory_space=pltpu.VMEM)
    smem = pl.BlockSpec(memory_space=pltpu.SMEM)
    hbm = pl.BlockSpec(memory_space=pl.ANY)
    result = pl.pallas_call(
        functools.partial(kernel, nz, ny, nx, cap),
        out_shape=jax.ShapeDtypeStruct((2, ny, 2, nz, 8, half_wide), f32),
        in_specs=[hbm, vmem, smem, vmem, smem],
        out_specs=hbm,
        scratch_shapes=[
            pltpu.VMEM((2, ny, 2, nz, 8, length), f32),
            pltpu.VMEM((nz, 2, ny, 8, length), f32),
            pltpu.VMEM((ny, 2, nz, 8, length), f32),
            pltpu.VMEM((nz, 2, 1, cap), i32),
            pltpu.VMEM((ny, 1, cap), i32),
            pltpu.VMEM((ny, 8, cap), f32),
            pltpu.VMEM((nz, 8, cap), f32),
            pltpu.VMEM((ny, 8, cap), f32),
            pltpu.VMEM((nz, 8, cap), f32),
            pltpu.VMEM((ny, nz, 8, cap), f32),
            pltpu.VMEM((nz, ny, 8, cap), f32),
            pltpu.VMEM((2, nz, 8, cap), f32),
            pltpu.VMEM((4 * half_wide, cap), bf16),
            pltpu.VMEM((2 * length, cap), bf16),
            pltpu.VMEM((2, ny, 2, nz, 8, half_wide), f32),
            pltpu.VMEM((ny, 2, nz, 8, half_wide), f32),
            dma(()),
            dma((2,)),
            dma((2, m, 2)),
            dma((2, m, 2)),
            dma((nz, 2)),
            dma((nz, 2)),
            dma((ny,)),
            dma((ny,)),
            dma((2, m)),
            dma((2, m)),
            dma((2, m)),
            dma((2, m)),
            dma((nz,)),
            dma((nz,)),
            dma((2, nx)),
            dma((2, nx)),
            dma((2,)),
            dma((2,)),
            dma((2, 2, m // 2)),
            dma((2, 2, m // 2)),
            dma((2, m)),
            dma((2, m)),
        ],
        compiler_params=pltpu.CompilerParams(collective_id=0, has_side_effects=True),
        name="sketch_gram",
    )(
        hidden_panel.reshape(2, ny, 2, nz, 8, length),
        row_signs.reshape(1, length),
        sample_rows,
        sample_counts.reshape(1, shards),
        ridge_weight.reshape(1, 1),
    )
    return result.reshape(width, half_wide)


def solution(mesh):
    placed = (P("cols", "rows"), P("rows"), P("rows", None), P(), P())
    return jax.shard_map(
        body, mesh=mesh, in_specs=placed, out_specs=P("cols", "rows"), check_vma=False
    )
```

time: 381 us -> 70.6 us (0.19)
  waiting for transfers between devices: 291 us -> 0 us
  Pallas kernels: 0 us -> 67.4 us
  starting transfers between devices: 44.5 us -> 0 us
  between operations: 14.9 us -> 0.66 us
  blocking collectives: 9.46 us -> 0 us
  matrix products: 8.04 us -> 0 us
  local copies, waits for them, and re-layouts: 8.41 us -> 2.34 us
  other arithmetic: 3.98 us -> 0 us
    ppermute x7 -> x0, waiting for transfers between devices: 235 us -> none  [swapped(): return lax.ppermute(value, axis, pairs)]
    pallas_call x0 -> x1, Pallas kernels: none -> 67.4 us  [body(): pl.pallas_call(functools.partial(kernel, nz, ny, nx, cap), out_shape=jax....]
    all_gather x1 -> x0, waiting for transfers between devices: 45.1 us -> none  [body(): all_slots = lax.all_gather(sketch, 'rows', axis=1, tiled=True)]
    ppermute x7 -> x0, starting transfers between devices: 29.4 us -> none  [swapped(): return lax.ppermute(value, axis, pairs)]
    all_to_all x1 -> x0, starting transfers between devices: 15 us -> none  [body(): lax.all_to_all(all_units, 'rows', split_axis=0, concat_axis=1, tiled=True)]
    all_to_all x1 -> x0, waiting for transfers between devices: 11.1 us -> none  [body(): lax.all_to_all(all_units, 'rows', split_axis=0, concat_axis=1, tiled=True)]
    all_gather x1 -> x0, blocking collectives: 9.46 us -> none  [body(): all_units = lax.all_gather(sketch, 'cols', axis=0, tiled=True)]
    dot_general x2 -> x0, matrix products: 8.04 us -> none  [the longest x1 5.77 us: body(): jnp.dot(all_slots, block_units.T, precision=lax.Precision.HIGHEST, prefer...]
  transfers between devices with their start and end apart: 9 -> 0, of which waited for: 9 -> 0; matrix products, arithmetic and copies ran while one was open for 1% -> 0% of each run, Pallas kernels for 0% -> 0%
where the time goes in v1:
time: 70.6 us; the launch traced here: 70.4 us
  Pallas kernels  67.4 us (95%)
  local copies, waits for them, and re-layouts  2.34 us (3%)
    pallas_call x1, Pallas kernels, body(): pl.pallas_call(functools.partial(kernel, nz, ny, nx, cap), out_shape=jax....  67.4 us
    reshape x1, local copies, waits for them, and re-layouts, body(): return result.reshape(width, half_wide)  2.34 us

profile of v1, /device:TPU:1, one launch (start us, length us, event | category | flops | bytes accessed | tf_op | source)
XLA Modules:
  0.0 70.4 jit_solution(12727614678416990554)
XLA Ops:
  0.7 67.4 %sketch_gram.1 = f32[2,8,2,8,8,64]{5,4,3,2,1,0:T(8,128)} custom-call(f32[2,8,2,8,8,128]{5,4,3,2,1,0:T(8,128)} %bitcast.7, f32[1,128]{1,0:T(1,128)} %bitcast.8, s32[1,4]{1,0:T(1,128)} %rows.1, s32[1,128]{1,0:T(1,128)} %bitcast.9, f32[1,1]{1,0:T(1,128)} %bitcast.5.ridge), custom_call_target="tpu_custom_call" | custom-call | tf_op jit(solution)/shard_map/sketch_gram/pallas_call | solution.py:400
  68.0 2.3 %copy.6 = f32[2048,64]{0,1:T(8,128)} copy(f32[2048,64]{1,0:T(8,128)} %bitcast.6) | data formatting | bytes 1048576 | tf_op jit(solution)/shard_map/reshape | solution.py:454

commit v2 on v1

v2 whole, which is shorter than its diff:
```python
import functools
import math

import jax
import jax.numpy as jnp
from jax import lax
from jax.experimental import pallas as pl
from jax.experimental.pallas import tpu as pltpu
from jax.sharding import PartitionSpec as P

MESH = pl.DeviceIdType.MESH


def halves(value):
    high = value.astype(jnp.bfloat16)
    return high, (value - high.astype(jnp.float32)).astype(jnp.bfloat16)


def signs_of(common):
    for shift in (8, 4, 2, 1):
        common = common ^ (common >> shift)
    return (1 - 2 * (common & 1)).astype(jnp.float32)


def far_first(n):
    return [n // 2] + [d for k in range(n // 2 - 1, 0, -1) for d in (k, n - k)]


def near_first(n):
    return [d for k in range(1, n // 2) for d in (k, n - k)] + [n // 2]


SUBS = 4
GROUP = 4
PLAN = (((1, 3), "relay0"), ((2, 1), "relay1"), ((2, 3), "far0"), ((3, 0), "far1"), ((3, 2), "ready"))


def kernel(
    nz, ny, nx, cap, panel, signs, rows, counts, ridge, out,
    xs, ra, rb, sm1, sm2, pa, pb, qa, qb, sa, sb, bo, b2, hh, ob, st,
    in_sem, out_sem, s_raw, r_raw, s_sm1, r_sm1, s_sm2, r_sm2, s_red, r_red, s_ag, r_ag,
    s_op, r_op, s_x, r_x, s_sib, r_sib, s_ring, r_ring, s_out, r_out,
):
    length = panel.shape[-1]
    shards = counts.shape[1]
    me = lax.axis_index("rows")
    q = lax.axis_index("cols")
    c = lax.rem(me, 2)
    y = lax.rem(me // 2, ny)
    z = me // (2 * ny)
    mate = 1 - c

    def at(zz, yy, cc, xx):
        return ((zz * ny + yy) * 2 + cc, xx)

    def up_z(d):
        return lax.rem(z + d, nz)

    def up_y(d):
        return lax.rem(y + d, ny)

    pending = []

    def send(src, dst, ss, rs, to, keep=True):
        copy = pltpu.make_async_remote_copy(
            src_ref=src, dst_ref=dst, send_sem=ss, recv_sem=rs, device_id=to, device_id_type=MESH
        )
        copy.start()
        if keep:
            pending.append(copy)
        return copy

    def arrived(slot, sem):
        pltpu.make_async_copy(slot, slot, sem).wait()

    def sent(src, sem):
        pltpu.make_async_copy(src, src, sem).wait()

    load = pltpu.make_async_copy(panel, xs, in_sem)
    load.start()

    barrier = pltpu.get_barrier_semaphore()
    greeted = [at(z, y, mate, q)]
    for d in range(1, nz):
        greeted += [at(up_z(d), y, cc, q) for cc in (0, 1)]
    for d in range(1, ny):
        greeted += [at(z, up_y(d), cc, q) for cc in (0, 1)]
    for d in range(1, nx):
        greeted.append(at(z, y, c, lax.rem(q + d, nx)))
    for to in greeted:
        pl.semaphore_signal(barrier, inc=1, device_id=to, device_id_type=MESH)

    count_row = counts[...].astype(jnp.float32)
    lane = lax.broadcasted_iota(jnp.int32, (shards, shards), 1)
    line = lax.broadcasted_iota(jnp.int32, (shards, shards), 0)
    ends = jnp.sum(jnp.where(lane <= line, count_row, 0.0), axis=1, keepdims=True)
    slot = lax.broadcasted_iota(jnp.int32, (1, cap), 1)
    passed = ends <= slot.astype(jnp.float32)
    pk = jnp.sum(passed.astype(jnp.float32), axis=0, keepdims=True).astype(jnp.int32)
    block = lax.broadcasted_iota(jnp.int32, (1, shards), 1)
    before = jnp.sum(jnp.where(block < me, count_row, 0.0), axis=1, keepdims=True)
    total = jnp.sum(count_row, axis=1, keepdims=True)
    place = slot - before.astype(jnp.int32)
    own = jnp.zeros((1, cap), jnp.int32)
    for j in range(rows.shape[1]):
        own = jnp.where((pk == me) & (place == j), rows[0, j] - me * length, own)
    sm1[z, c] = own

    load.wait()
    xs[...] = xs[...] * signs[...]
    pl.semaphore_wait(barrier, len(greeted))

    @pl.when(c == 0)
    def _():
        send(sm1.at[z, 0], sm1.at[z, 0], s_sm1.at[0], r_sm1.at[0, 0], at(z, y, 1, q), keep=False)

    for d in range(1, nz):
        send(sm1.at[z, c], sm1.at[z, c], s_sm1.at[d], r_sm1.at[d, c], at(up_z(d), y, 1, q))

    def raw_z(d):
        for cc in (0, 1):
            send(xs.at[cc, :, 0, up_z(d)], ra.at[z, c], s_raw.at[0, d, cc], r_raw.at[0, d, c], at(up_z(d), y, cc, q), keep=False)

    def raw_y(d):
        for cc in (0, 1):
            send(xs.at[cc, up_y(d), 1], rb.at[y, c], s_raw.at[1, d, cc], r_raw.at[1, d, c], at(z, up_y(d), cc, q), keep=False)

    order_z, order_y = near_first(nz), near_first(ny)

    @pl.when(c == 0)
    def _():
        for k in range(max(len(order_z), len(order_y))):
            if k < len(order_z):
                raw_z(order_z[k])
            if k < len(order_y):
                raw_y(order_y[k])

    @pl.when(c == 1)
    def _():
        for d in order_z:
            raw_z(d)
        arrived(sm1.at[z, 0], r_sm1.at[0, 0])
        for d in range(1, nz):
            for cc in (0, 1):
                arrived(sm1.at[up_z(nz - d), cc], r_sm1.at[d, cc])
        sm2[y] = jnp.sum(sm1[...].reshape(2 * nz, 1, cap), axis=0)
        for d in range(1, ny):
            for cc in (0, 1):
                send(sm2.at[y], sm2.at[y], s_sm2.at[d, cc], r_sm2.at[d], at(z, up_y(d), cc, q), keep=False)
        send(sm2.at[y], sm2.at[y], s_sm2.at[0, 0], r_sm2.at[0], at(z, y, 0, q), keep=False)
        for d in order_y:
            raw_y(d)

    send(xs.at[mate, :, 0, z], ra.at[z, c], s_raw.at[0, 0, 0], r_raw.at[0, 0, c], at(z, y, mate, q))
    send(xs.at[mate, y, 1], rb.at[y, c], s_raw.at[1, 0, 0], r_raw.at[1, 0, c], at(z, y, mate, q))

    @pl.when(c == 0)
    def _():
        arrived(sm2.at[y], r_sm2.at[0])

    for d in range(1, ny):
        arrived(sm2.at[up_y(ny - d)], r_sm2.at[d])
    local_row = jnp.sum(sm2[...], axis=0)

    token = lax.broadcasted_iota(jnp.int32, (length, cap), 0)
    scale = 1.0 / math.sqrt(length * shards)
    live = jnp.where(slot.astype(jnp.float32) < total, scale, 0.0)
    sign = (signs_of(token & local_row) * live).astype(jnp.bfloat16)
    hh[:length] = sign
    hh[length:] = sign

    def share(parts, acc):
        pieces = [jnp.concatenate(halves(value), axis=1) for value, _ in parts]
        made = jnp.dot(jnp.concatenate(pieces, axis=0), hh[...], preferred_element_type=jnp.float32)
        high = made.shape[0] // len(parts)
        for k, (_, source) in enumerate(parts):
            term = made[k * high : (k + 1) * high] * signs_of(pk & source)
            acc = term if acc is None else acc + term
        return acc

    def batches(n):
        return [(0,)] + [(d, n - d) for d in range(1, n // 2)] + [(n // 2,)]

    def flat(value):
        return value.reshape(-1, value.shape[-1])

    def block_of(zz, yy, cc):
        return (zz * ny + yy) * 2 + cc

    def share_of(which, batch, acc):
        n, mine, buf = (nz, z, ra) if which == 0 else (ny, y, rb)
        parts = []
        for d in batch:
            far = lax.rem(mine + n - d, n) if d else mine
            for cc in (0, 1):
                if d == 0 and cc == 0:
                    held = xs[c, :, 0, z] if which == 0 else xs[c, y, 1]
                    parts.append((flat(held), block_of(z, y, c)))
                    continue
                source = mate if d == 0 else cc
                arrived(buf.at[far, source], r_raw.at[which, d, source])
                block_at = block_of(far, y, source) if which == 0 else block_of(z, far, source)
                parts.append((flat(buf[far, source]), block_at))
        return share(parts, acc)

    steps_z, steps_y = batches(nz), batches(ny)
    acc_z = acc_y = None
    for k in range(max(len(steps_z), len(steps_y))):
        if k < len(steps_z):
            acc_z = share_of(0, steps_z[k], acc_z)
            if k == len(steps_z) - 1:
                pa[...] = acc_z.reshape(ny, 8, cap)
                for d in far_first(ny):
                    send(pa.at[up_y(d)], qa.at[y], s_red.at[0, d], r_red.at[0, d], at(z, up_y(d), c, q))
        if k < len(steps_y):
            acc_y = share_of(1, steps_y[k], acc_y)
            if k == len(steps_y) - 1:
                pb[...] = acc_y.reshape(nz, 8, cap)
                for d in far_first(nz):
                    send(pb.at[up_z(d)], qb.at[z], s_red.at[1, d], r_red.at[1, d], at(up_z(d), y, c, q))

    subs = min(SUBS, nz, ny)

    def hold(which, d, k):
        n, mine, buf = (ny, y, sa) if which == 0 else (nz, z, sb)
        size = buf.shape[1] // subs
        return buf.at[lax.rem(mine + d, n), pl.ds(k * size, size)]

    extent = (ny, nz)

    def come_from(which, way, d):
        return (extent[which] - d) % extent[which] if way == 0 else d

    def passes(which, way, d, k):
        n = extent[which]
        return d < n // 2 or (d == n // 2 and k % 2 == way)

    def pass_on(which, d, k, ways=(0, 1)):
        n = extent[which]
        for way in ways:
            if not passes(which, way, d + 1, k):
                continue
            view = hold(which, come_from(which, way, d), k)
            step = 1 if way == 0 else n - 1
            to = at(z, up_y(step), c, q) if which == 0 else at(up_z(step), y, c, q)
            send(view, view, s_ring.at[which, way, d, k], r_ring.at[which, way, d, k], to)

    def take(which, d, k):
        for way in (0, 1):
            if passes(which, way, d, k):
                view = hold(which, come_from(which, way, d), k)
                arrived(view, r_ring.at[which, way, d - 1, k])
                pass_on(which, d, k, (way,))

    target = 2 * q + c
    hop = lax.rem(target - z + nz, nz)

    piece = pa[y]
    for d in range(1, ny):
        arrived(qa.at[up_y(ny - d)], r_red.at[0, d])
        piece = piece + qa[up_y(ny - d)]
    sa[y, z] = piece
    for d in far_first(nz):
        send(sa.at[y, z], sa.at[y, z], s_ag.at[0, d], r_ag.at[0, d], at(up_z(d), y, c, q))
    piece = pb[z]
    for d in range(1, nz):
        arrived(qb.at[up_z(nz - d)], r_red.at[1, d])
        piece = piece + qb[up_z(nz - d)]
    sb[z, y] = piece

    @pl.when(hop != 0)
    def _():
        send(sb.at[z, y], bo.at[1, z], s_op.at[hop], r_op.at[hop], at(target, y, c, q), keep=False)

    @pl.when(hop == 0)
    def _():
        bo[1, z] = piece

    for d in far_first(ny):
        send(sb.at[z, y], sb.at[z, y], s_ag.at[1, d], r_ag.at[1, d], at(z, up_y(d), c, q))
    for e in range(1, nz):
        arrived(sa.at[y, up_z(nz - e)], r_ag.at[0, e])
    for k in range(subs):
        pass_on(0, 0, k)
    for e in range(1, ny):
        arrived(sb.at[z, up_y(ny - e)], r_ag.at[1, e])
    for k in range(subs):
        pass_on(1, 0, k)

    root_c = lax.rem(z, 2)
    root_q = z // 2
    away = lax.rem(q - root_q + nx, nx)
    beside = [d for d in (1, nx - 1) if d] if nx > 2 else [1]
    mid = nz // 2

    @pl.when((c == root_c) & (away == 0))
    def _():
        for d in beside:
            send(sa.at[y], bo.at[0], s_x.at[0, d], r_x.at[0, 0], at(z, y, c, lax.rem(q + d, nx)), keep=False)
        send(sa.at[y], bo.at[0], s_sib.at[0], r_sib.at[0], at(z, y, mate, q), keep=False)
        for d in range(1, nz):
            arrived(bo.at[1, up_z(nz - d)], r_op.at[d])
        for d in beside:
            send(bo.at[1], bo.at[1], s_x.at[1, d], r_x.at[1, 0], at(z, y, c, lax.rem(q + d, nx)), keep=False)
        send(bo.at[1], bo.at[1], s_sib.at[1], r_sib.at[1], at(z, y, mate, q), keep=False)
        bo[0] = sa[y]

    def relay(h):
        for d in beside:
            part = pl.ds(0 if d == 1 else mid, mid)

            @pl.when((c == root_c) & (away == d))
            def _():
                arrived(bo.at[h], r_x.at[h, 0])
                if nx > 2:
                    there = lax.rem(root_q + 2, nx)
                    view = bo.at[h, part]
                    send(view, view, s_x.at[h, 2], r_x.at[h, d], at(z, y, c, there), keep=False)
                send(bo.at[h], bo.at[h], s_sib.at[h], r_sib.at[h], at(z, y, mate, q), keep=False)

    def relay_far(h):
        if nx > 2:

            @pl.when((c == root_c) & (away == 2))
            def _():
                for d in beside:
                    view = bo.at[h, pl.ds(0 if d == 1 else mid, mid)]
                    arrived(view, r_x.at[h, d])
                send(bo.at[h], bo.at[h], s_sib.at[h], r_sib.at[h], at(z, y, mate, q), keep=False)

    wide = 2 * nz * 8
    half_wide = wide // 2

    now_ready = [False]

    def columns_ready():
        @pl.when(c != root_c)
        def _():
            for h in (0, 1):
                arrived(bo.at[h], r_sib.at[h])

        b_high, b_low = halves(flat(bo[...].reshape(2 * nz, 8, cap)))
        b2[:, :wide] = b_high.T
        b2[:, wide:] = b_low.T

    def ready_now():
        columns_ready()
        now_ready[0] = True

    def tail_relays():
        for name in ("relay0", "relay1", "far0", "far1"):
            if name not in acted:
                act_of[name]()
        ready_now()

    acted = set()

    def once(name, act):
        def run():
            if name not in acted:
                acted.add(name)
                act()

        return run

    act_of = {
        "relay0": once("relay0", lambda: relay(0)),
        "relay1": once("relay1", lambda: relay(1)),
        "far0": once("far0", lambda: relay_far(0)),
        "far1": once("far1", lambda: relay_far(1)),
        "ready": once("ready", tail_relays),
    }

    units = 2 * ny * wide
    first = q * units + c * (ny * wide)
    col = (z * ny + y) * wide + lax.broadcasted_iota(jnp.int32, (1, wide), 1)
    inverse = 1.0 / total
    weight = ridge[0, 0]

    def emit(group):
        pieces, rows_of = [], []
        for which, d in group:
            n, mine = (ny, y) if which == 0 else (nz, z)
            chunk = lax.rem(mine + d, n)
            value = flat(sa[chunk] if which == 0 else sb[chunk])
            pieces += halves(value)
            r = lax.broadcasted_iota(jnp.int32, (value.shape[0], 1), 0)
            if which == 0:
                unit = first + chunk * wide + r
            else:
                unit = first + (r // 8) * wide + half_wide + chunk * 8 + lax.rem(r, 8)
            rows_of.append((which, chunk, unit))
        made = jnp.dot(jnp.concatenate(pieces, axis=0), b2[...], preferred_element_type=jnp.float32)
        made = made[:, :wide] + made[:, wide:]
        at_row = 0
        for which, chunk, unit in rows_of:
            high = unit.shape[0]
            part = made[at_row : at_row + high] + made[at_row + high : at_row + 2 * high]
            at_row += 2 * high
            part = (part * inverse + jnp.where(unit == col, weight, 0.0)).reshape(-1, 8, wide)
            if which == 0:
                ob[chunk, 0] = part
            else:
                ob[:, 1, chunk] = part

    work = [(1, 0), (0, 0)]
    for d in range(1, max(ny, nz) // 2):
        for which in (1, 0):
            if d < extent[which] // 2:
                work += [(which, d), (which, extent[which] - d)]

    top = max(ny, nz) // 2
    done = 0
    for d in range(1, top + 1):
        for k in range(subs):
            for which in (0, 1):
                if d <= extent[which] // 2:
                    take(which, d, k)
            for now, act in PLAN:
                if now == (d, k):
                    act_of[act]()
            able = [w for w in work[done:] if min(w[1], extent[w[0]] - w[1]) < d]
            if now_ready[0] and able:
                emit(able[:GROUP])
                done += len(able[:GROUP])
    if not now_ready[0]:
        act_of["ready"]()
    while done < len(work):
        emit(work[done : done + GROUP])
        done += GROUP
    emit([(which, extent[which] // 2) for which in (1, 0)])

    puts = []
    for k in range(ny):
        st[k] = ob[k].reshape(wide, wide).T.reshape(2, half_wide, wide)
        lanes = pl.ds(pl.multiple_of((c * ny + k) * wide, wide), wide)
        send(st.at[k, mate], out.at[:, lanes], s_out.at[k], r_out.at[k], at(z, y, mate, q))
        put = pltpu.make_async_copy(st.at[k, c], out.at[:, lanes], out_sem.at[k])
        put.start()
        puts.append(put)
    for k in range(ny):
        lanes = pl.ds(pl.multiple_of((mate * ny + k) * wide, wide), wide)
        arrived(out.at[:, lanes], r_out.at[k])
    for put in puts:
        put.wait()

    for copy in pending:
        copy.wait_send()
    for d in range(1, nz):
        for cc in (0, 1):
            sent(ra.at[0, 0], s_raw.at[0, d, cc])
    for d in range(1, ny):
        for cc in (0, 1):
            sent(rb.at[0, 0], s_raw.at[1, d, cc])

    @pl.when(c == 0)
    def _():
        sent(sm1.at[0, 0], s_sm1.at[0])

    @pl.when(c == 1)
    def _():
        for d in range(1, ny):
            for cc in (0, 1):
                sent(sm2.at[0], s_sm2.at[d, cc])
        sent(sm2.at[0], s_sm2.at[0, 0])

    @pl.when(hop != 0)
    def _():
        sent(sb.at[z, y], s_op.at[hop])

    @pl.when((c == root_c) & (away == 0))
    def _():
        for h in (0, 1):
            for d in beside:
                sent(bo.at[h], s_x.at[h, d])

    if nx > 2:

        @pl.when((c == root_c) & (lax.rem(away, 2) == 1))
        def _():
            for h in (0, 1):
                sent(bo.at[h, pl.ds(0, mid)], s_x.at[h, 2])

    @pl.when(c == root_c)
    def _():
        for h in (0, 1):
            sent(bo.at[h], s_sib.at[h])


def body(hidden_panel, row_signs, sample_rows, sample_counts, ridge_weight):
    nx = lax.axis_size("cols")
    nz = 2 * nx
    ny = lax.axis_size("rows") // (2 * nz)
    width, length = hidden_panel.shape
    shards = sample_counts.shape[0]
    cap = -(-shards * sample_rows.shape[1] // 128) * 128
    half_wide = 8 * nz
    dma, f32, i32, bf16 = pltpu.SemaphoreType.DMA, jnp.float32, jnp.int32, jnp.bfloat16
    m = max(nz, ny)
    vmem = pl.BlockSpec(memory_space=pltpu.VMEM)
    smem = pl.BlockSpec(memory_space=pltpu.SMEM)
    hbm = pl.BlockSpec(memory_space=pl.ANY)
    result = pl.pallas_call(
        functools.partial(kernel, nz, ny, nx, cap),
        out_shape=jax.ShapeDtypeStruct((half_wide, width), f32),
        in_specs=[hbm, vmem, smem, vmem, smem],
        out_specs=hbm,
        scratch_shapes=[
            pltpu.VMEM((2, ny, 2, nz, 8, length), f32),
            pltpu.VMEM((nz, 2, ny, 8, length), f32),
            pltpu.VMEM((ny, 2, nz, 8, length), f32),
            pltpu.VMEM((nz, 2, 1, cap), i32),
            pltpu.VMEM((ny, 1, cap), i32),
            pltpu.VMEM((ny, 8, cap), f32),
            pltpu.VMEM((nz, 8, cap), f32),
            pltpu.VMEM((ny, 8, cap), f32),
            pltpu.VMEM((nz, 8, cap), f32),
            pltpu.VMEM((ny, nz, 8, cap), f32),
            pltpu.VMEM((nz, ny, 8, cap), f32),
            pltpu.VMEM((2, nz, 8, cap), f32),
            pltpu.VMEM((cap, 4 * half_wide), bf16),
            pltpu.VMEM((2 * length, cap), bf16),
            pltpu.VMEM((ny, 2, nz, 8, 2 * half_wide), f32),
            pltpu.VMEM((ny, 2, half_wide, 2 * half_wide), f32),
            dma(()),
            dma((ny,)),
            dma((2, m, 2)),
            dma((2, m, 2)),
            dma((nz,)),
            dma((nz, 2)),
            dma((ny, 2)),
            dma((ny,)),
            dma((2, m)),
            dma((2, m)),
            dma((2, m)),
            dma((2, m)),
            dma((nz,)),
            dma((nz,)),
            dma((2, nx)),
            dma((2, nx)),
            dma((2,)),
            dma((2,)),
            dma((2, 2, m // 2, m)),
            dma((2, 2, m // 2, m)),
            dma((ny,)),
            dma((ny,)),
        ],
        compiler_params=pltpu.CompilerParams(collective_id=0, has_side_effects=True),
        name="sketch_gram",
    )(
        hidden_panel.reshape(2, ny, 2, nz, 8, length),
        row_signs.reshape(1, length),
        sample_rows,
        sample_counts.reshape(1, shards),
        ridge_weight.reshape(1, 1),
    )
    return result.T


def solution(mesh):
    placed = (P("cols", "rows"), P("rows"), P("rows", None), P(), P())
    return jax.shard_map(
        body, mesh=mesh, in_specs=placed, out_specs=P("cols", "rows"), check_vma=False
    )
```

time: 70.6 us -> 67.5 us (0.956)
  Pallas kernels: 67.4 us -> 64.7 us
    pallas_call x1, Pallas kernels: 67.4 us -> 64.7 us  [body(): pl.pallas_call(functools.partial(kernel, nz, ny, nx, cap), out_shape=jax....]
    reshape x1 -> x0, local copies, waits for them, and re-layouts: 2.34 us -> none  [body(): return result.reshape(width, half_wide)]
    unnamed x0 -> x1, local copies, waits for them, and re-layouts: none -> 1.87 us
where the time goes in v2:
time: 67.5 us; the launch traced here: 67.3 us
  Pallas kernels  64.7 us (96%)
  local copies, waits for them, and re-layouts  1.87 us (3%)
    pallas_call x1, Pallas kernels, body(): pl.pallas_call(functools.partial(kernel, nz, ny, nx, cap), out_shape=jax....  64.7 us
    unnamed x1, local copies, waits for them, and re-layouts  1.87 us

profile of v2, /device:TPU:1, one launch (start us, length us, event | category | flops | bytes accessed | tf_op | source)
XLA Modules:
  0.0 67.3 jit_solution(6341528818556887459)
XLA Ops:
  0.7 64.7 %sketch_gram.1 = f32[64,2048]{1,0:T(8,128)} custom-call(f32[2,8,2,8,8,128]{5,4,3,2,1,0:T(8,128)} %bitcast.7, f32[1,128]{1,0:T(1,128)} %bitcast.8, s32[1,4]{1,0:T(1,128)} %rows.1, s32[1,128]{1,0:T(1,128)} %bitcast.9, f32[1,1]{1,0:T(1,128)} %bitcast.5.ridge), custom_call_target="tpu_custom_call" | custom-call | tf_op jit(solution)/shard_map/sketch_gram/pallas_call | solution.py:503
  65.4 1.9 %copy.8 = f32[2048,64]{0,1:T(8,128)} copy(f32[2048,64]{0,1:T(8,128)} %bitcast.6) | data formatting | bytes 1048576

commit v3 on v2

--- a/solution.py
+++ b/solution.py
@@ -16,6 +16,10 @@
     return high, (value - high.astype(jnp.float32)).astype(jnp.bfloat16)
 
 
+def wrap(value, n):
+    return value & (n - 1) if n & (n - 1) == 0 else lax.rem(value, n)
+
+
 def signs_of(common):
     for shift in (8, 4, 2, 1):
         common = common ^ (common >> shift)
@@ -37,27 +41,27 @@
 
 def kernel(
     nz, ny, nx, cap, panel, signs, rows, counts, ridge, out,
-    xs, ra, rb, sm1, sm2, pa, pb, qa, qb, sa, sb, bo, b2, hh, ob, st,
-    in_sem, out_sem, s_raw, r_raw, s_sm1, r_sm1, s_sm2, r_sm2, s_red, r_red, s_ag, r_ag,
+    xs, ra, rb, sm1, sm2, pa, pb, qa, qb, sa, sb, bo, bn, b2, hh, ob, st,
+    in_sem, s_raw, r_raw, s_sm1, r_sm1, s_sm2, r_sm2, s_red, r_red, s_ag, r_ag,
     s_op, r_op, s_x, r_x, s_sib, r_sib, s_ring, r_ring, s_out, r_out,
 ):
     length = panel.shape[-1]
     shards = counts.shape[1]
     me = lax.axis_index("rows")
     q = lax.axis_index("cols")
-    c = lax.rem(me, 2)
-    y = lax.rem(me // 2, ny)
-    z = me // (2 * ny)
+    c = wrap(me, 2)
+    y = wrap(me >> 1, ny)
+    z = (me >> 1) // ny if ny & (ny - 1) else me >> ny.bit_length()
     mate = 1 - c
 
     def at(zz, yy, cc, xx):
         return ((zz * ny + yy) * 2 + cc, xx)
 
     def up_z(d):
-        return lax.rem(z + d, nz)
+        return wrap(z + d, nz)
 
     def up_y(d):
-        return lax.rem(y + d, ny)
+        return wrap(y + d, ny)
 
     pending = []
 
@@ -86,7 +90,7 @@
     for d in range(1, ny):
         greeted += [at(z, up_y(d), cc, q) for cc in (0, 1)]
     for d in range(1, nx):
-        greeted.append(at(z, y, c, lax.rem(q + d, nx)))
+        greeted.append(at(z, y, c, wrap(q + d, nx)))
     for to in greeted:
         pl.semaphore_signal(barrier, inc=1, device_id=to, device_id_type=MESH)
 
@@ -125,6 +129,9 @@
         for cc in (0, 1):
             send(xs.at[cc, up_y(d), 1], rb.at[y, c], s_raw.at[1, d, cc], r_raw.at[1, d, c], at(z, up_y(d), cc, q), keep=False)
 
+    send(xs.at[mate, :, 0, z], ra.at[z, c], s_raw.at[0, 0, 0], r_raw.at[0, 0, c], at(z, y, mate, q))
+    send(xs.at[mate, y, 1], rb.at[y, c], s_raw.at[1, 0, 0], r_raw.at[1, 0, c], at(z, y, mate, q))
+
     order_z, order_y = near_first(nz), near_first(ny)
 
     @pl.when(c == 0)
@@ -151,9 +158,6 @@
         for d in order_y:
             raw_y(d)
 
-    send(xs.at[mate, :, 0, z], ra.at[z, c], s_raw.at[0, 0, 0], r_raw.at[0, 0, c], at(z, y, mate, q))
-    send(xs.at[mate, y, 1], rb.at[y, c], s_raw.at[1, 0, 0], r_raw.at[1, 0, c], at(z, y, mate, q))
-
     @pl.when(c == 0)
     def _():
         arrived(sm2.at[y], r_sm2.at[0])
@@ -191,7 +195,7 @@
         n, mine, buf = (nz, z, ra) if which == 0 else (ny, y, rb)
         parts = []
         for d in batch:
-            far = lax.rem(mine + n - d, n) if d else mine
+            far = wrap(mine + n - d, n) if d else mine
             for cc in (0, 1):
                 if d == 0 and cc == 0:
                     held = xs[c, :, 0, z] if which == 0 else xs[c, y, 1]
@@ -224,9 +228,10 @@
     def hold(which, d, k):
         n, mine, buf = (ny, y, sa) if which == 0 else (nz, z, sb)
         size = buf.shape[1] // subs
-        return buf.at[lax.rem(mine + d, n), pl.ds(k * size, size)]
+        return buf.at[wrap(mine + d, n), pl.ds(k * size, size)]
 
     extent = (ny, nz)
+    orders = ([0] + near_first(nz), [0] + near_first(ny))
 
     def come_from(which, way, d):
         return (extent[which] - d) % extent[which] if way == 0 else d
@@ -237,13 +242,15 @@
 
     def pass_on(which, d, k, ways=(0, 1)):
         n = extent[which]
+        leap = min(2, n // 2)
         for way in ways:
-            if not passes(which, way, d + 1, k):
-                continue
             view = hold(which, come_from(which, way, d), k)
-            step = 1 if way == 0 else n - 1
-            to = at(z, up_y(step), c, q) if which == 0 else at(up_z(step), y, c, q)
-            send(view, view, s_ring.at[which, way, d, k], r_ring.at[which, way, d, k], to)
+            for far in ([d + 1] if d + 1 < n // 2 else []) + ([n // 2] if d == n // 2 - leap else []):
+                if not passes(which, way, far, k):
+                    continue
+                step = far - d if way == 0 else n - (far - d)
+                to = at(z, up_y(step), c, q) if which == 0 else at(up_z(step), y, c, q)
+                send(view, view, s_ring.at[which, way, far - 1, k], r_ring.at[which, way, far - 1, k], to)
 
     def take(which, d, k):
         for way in (0, 1):
@@ -253,55 +260,56 @@
                 pass_on(which, d, k, (way,))
 
     target = 2 * q + c
-    hop = lax.rem(target - z + nz, nz)
+    hop = wrap(target - z + nz, nz)
 
     piece = pa[y]
     for d in range(1, ny):
         arrived(qa.at[up_y(ny - d)], r_red.at[0, d])
         piece = piece + qa[up_y(ny - d)]
-    sa[y, z] = piece
-    for d in far_first(nz):
-        send(sa.at[y, z], sa.at[y, z], s_ag.at[0, d], r_ag.at[0, d], at(up_z(d), y, c, q))
+    sa[y, 0] = piece
+    for d in near_first(nz):
+        send(sa.at[y, 0], sa.at[y, orders[0].index(d)], s_ag.at[0, d], r_ag.at[0, d], at(up_z(d), y, c, q))
     piece = pb[z]
     for d in range(1, nz):
         arrived(qb.at[up_z(nz - d)], r_red.at[1, d])
         piece = piece + qb[up_z(nz - d)]
-    sb[z, y] = piece
+    sb[z, 0] = piece
 
     @pl.when(hop != 0)
     def _():
-        send(sb.at[z, y], bo.at[1, z], s_op.at[hop], r_op.at[hop], at(target, y, c, q), keep=False)
+        send(sb.at[z, 0], bo.at[1, z], s_op.at[hop], r_op.at[hop], at(target, y, c, q), keep=False)
 
     @pl.when(hop == 0)
     def _():
         bo[1, z] = piece
 
-    for d in far_first(ny):
-        send(sb.at[z, y], sb.at[z, y], s_ag.at[1, d], r_ag.at[1, d], at(z, up_y(d), c, q))
-    for e in range(1, nz):
-        arrived(sa.at[y, up_z(nz - e)], r_ag.at[0, e])
+    for d in near_first(ny):
+        send(sb.at[z, 0], sb.at[z, orders[1].index(d)], s_ag.at[1, d], r_ag.at[1, d], at(z, up_y(d), c, q))
     for k in range(subs):
-        pass_on(0, 0, k)
-    for e in range(1, ny):
-        arrived(sb.at[z, up_y(ny - e)], r_ag.at[1, e])
-    for k in range(subs):
-        pass_on(1, 0, k)
-
-    root_c = lax.rem(z, 2)
-    root_q = z // 2
-    away = lax.rem(q - root_q + nx, nx)
+        for which in (0, 1):
+            mine, buf = (y, sa) if which == 0 else (z, sb)
+            size = buf.shape[1] // subs
+            for place_of in range(k * size, (k + 1) * size):
+                e = orders[which][place_of]
+                if e:
+                    arrived(buf.at[mine, place_of], r_ag.at[which, e])
+            pass_on(which, 0, k)
+
+    root_c = wrap(z, 2)
+    root_q = z >> 1
+    away = wrap(q - root_q + nx, nx)
     beside = [d for d in (1, nx - 1) if d] if nx > 2 else [1]
     mid = nz // 2
 
     @pl.when((c == root_c) & (away == 0))
     def _():
         for d in beside:
-            send(sa.at[y], bo.at[0], s_x.at[0, d], r_x.at[0, 0], at(z, y, c, lax.rem(q + d, nx)), keep=False)
+            send(sa.at[y], bo.at[0], s_x.at[0, d], r_x.at[0, 0], at(z, y, c, wrap(q + d, nx)), keep=False)
         send(sa.at[y], bo.at[0], s_sib.at[0], r_sib.at[0], at(z, y, mate, q), keep=False)
         for d in range(1, nz):
             arrived(bo.at[1, up_z(nz - d)], r_op.at[d])
         for d in beside:
-            send(bo.at[1], bo.at[1], s_x.at[1, d], r_x.at[1, 0], at(z, y, c, lax.rem(q + d, nx)), keep=False)
+            send(bo.at[1], bo.at[1], s_x.at[1, d], r_x.at[1, 0], at(z, y, c, wrap(q + d, nx)), keep=False)
         send(bo.at[1], bo.at[1], s_sib.at[1], r_sib.at[1], at(z, y, mate, q), keep=False)
         bo[0] = sa[y]
 
@@ -313,7 +321,7 @@
             def _():
                 arrived(bo.at[h], r_x.at[h, 0])
                 if nx > 2:
-                    there = lax.rem(root_q + 2, nx)
+                    there = wrap(root_q + 2, nx)
                     view = bo.at[h, part]
                     send(view, view, s_x.at[h, 2], r_x.at[h, d], at(z, y, c, there), keep=False)
                 send(bo.at[h], bo.at[h], s_sib.at[h], r_sib.at[h], at(z, y, mate, q), keep=False)
@@ -339,7 +347,9 @@
             for h in (0, 1):
                 arrived(bo.at[h], r_sib.at[h])
 
-        b_high, b_low = halves(flat(bo[...].reshape(2 * nz, 8, cap)))
+        for k, e in enumerate(orders[0]):
+            bn[wrap(z + nz - e, nz)] = bo[0, k]
+        b_high, b_low = halves(jnp.concatenate([flat(bn[...]), flat(bo[1])], axis=0))
         b2[:, :wide] = b_high.T
         b2[:, wide:] = b_low.T
 
@@ -376,32 +386,29 @@
     col = (z * ny + y) * wide + lax.broadcasted_iota(jnp.int32, (1, wide), 1)
     inverse = 1.0 / total
     weight = ridge[0, 0]
+    line8 = lax.broadcasted_iota(jnp.int32, (8, 1), 0)
 
     def emit(group):
         pieces, rows_of = [], []
         for which, d in group:
             n, mine = (ny, y) if which == 0 else (nz, z)
-            chunk = lax.rem(mine + d, n)
+            chunk = wrap(mine + d, n)
             value = flat(sa[chunk] if which == 0 else sb[chunk])
             pieces += halves(value)
-            r = lax.broadcasted_iota(jnp.int32, (value.shape[0], 1), 0)
-            if which == 0:
-                unit = first + chunk * wide + r
-            else:
-                unit = first + (r // 8) * wide + half_wide + chunk * 8 + lax.rem(r, 8)
-            rows_of.append((which, chunk, unit))
+            rows_of.append((which, chunk, value.shape[0]))
         made = jnp.dot(jnp.concatenate(pieces, axis=0), b2[...], preferred_element_type=jnp.float32)
         made = made[:, :wide] + made[:, wide:]
         at_row = 0
-        for which, chunk, unit in rows_of:
-            high = unit.shape[0]
-            part = made[at_row : at_row + high] + made[at_row + high : at_row + 2 * high]
+        for which, chunk, high in rows_of:
+            part = (made[at_row : at_row + high] + made[at_row + high : at_row + 2 * high]) * inverse
             at_row += 2 * high
-            part = (part * inverse + jnp.where(unit == col, weight, 0.0)).reshape(-1, 8, wide)
-            if which == 0:
-                ob[chunk, 0] = part
-            else:
-                ob[:, 1, chunk] = part
+            for k, e in enumerate(orders[which]):
+                if which == 0:
+                    block, zz = chunk, wrap(z + nz - e, nz)
+                else:
+                    block, zz = wrap(y + ny - e, ny), chunk
+                unit = first + block * wide + which * half_wide + zz * 8 + line8
+                ob[block, which, zz] = part[k * 8 : (k + 1) * 8] + jnp.where(unit == col, weight, 0.0)
 
     work = [(1, 0), (0, 0)]
     for d in range(1, max(ny, nz) // 2):
@@ -430,19 +437,16 @@
         done += GROUP
     emit([(which, extent[which] // 2) for which in (1, 0)])
 
-    puts = []
     for k in range(ny):
-        st[k] = ob[k].reshape(wide, wide).T.reshape(2, half_wide, wide)
+        turned = ob[k].reshape(wide, wide).T
+        left, right = turned[:half_wide], turned[half_wide:]
         lanes = pl.ds(pl.multiple_of((c * ny + k) * wide, wide), wide)
-        send(st.at[k, mate], out.at[:, lanes], s_out.at[k], r_out.at[k], at(z, y, mate, q))
-        put = pltpu.make_async_copy(st.at[k, c], out.at[:, lanes], out_sem.at[k])
-        put.start()
-        puts.append(put)
+        st[k] = jnp.where(c == 0, right, left)
+        send(st.at[k], out.at[:, lanes], s_out.at[k], r_out.at[k], at(z, y, mate, q))
+        out[:, lanes] = jnp.where(c == 0, left, right)
     for k in range(ny):
         lanes = pl.ds(pl.multiple_of((mate * ny + k) * wide, wide), wide)
         arrived(out.at[:, lanes], r_out.at[k])
-    for put in puts:
-        put.wait()
 
     for copy in pending:
         copy.wait_send()
@@ -466,7 +470,7 @@
 
     @pl.when(hop != 0)
     def _():
-        sent(sb.at[z, y], s_op.at[hop])
+        sent(sb.at[z, 0], s_op.at[hop])
 
     @pl.when((c == root_c) & (away == 0))
     def _():
@@ -476,7 +480,7 @@
 
     if nx > 2:
 
-        @pl.when((c == root_c) & (lax.rem(away, 2) == 1))
+        @pl.when((c == root_c) & (wrap(away, 2) == 1))
         def _():
             for h in (0, 1):
                 sent(bo.at[h, pl.ds(0, mid)], s_x.at[h, 2])
@@ -502,9 +506,9 @@
     hbm = pl.BlockSpec(memory_space=pl.ANY)
     result = pl.pallas_call(
         functools.partial(kernel, nz, ny, nx, cap),
-        out_shape=jax.ShapeDtypeStruct((half_wide, width), f32),
+        out_shape=pltpu.VMEM((half_wide, width), f32),
         in_specs=[hbm, vmem, smem, vmem, smem],
-        out_specs=hbm,
+        out_specs=vmem,
         scratch_shapes=[
             pltpu.VMEM((2, ny, 2, nz, 8, length), f32),
             pltpu.VMEM((nz, 2, ny, 8, length), f32),
@@ -518,12 +522,12 @@
             pltpu.VMEM((ny, nz, 8, cap), f32),
             pltpu.VMEM((nz, ny, 8, cap), f32),
             pltpu.VMEM((2, nz, 8, cap), f32),
+            pltpu.VMEM((nz, 8, cap), f32),
             pltpu.VMEM((cap, 4 * half_wide), bf16),
             pltpu.VMEM((2 * length, cap), bf16),
             pltpu.VMEM((ny, 2, nz, 8, 2 * half_wide), f32),
-            pltpu.VMEM((ny, 2, half_wide, 2 * half_wide), f32),
+            pltpu.VMEM((ny, half_wide, 2 * half_wide), f32),
             dma(()),
-            dma((ny,)),
             dma((2, m, 2)),
             dma((2, m, 2)),
             dma((nz,)),

time: 67.5 us -> 65.1 us (0.964)
  Pallas kernels: 64.7 us -> 63.5 us
  local copies, waits for them, and re-layouts: 1.87 us -> 0.8 us
    pallas_call x1, Pallas kernels: 64.7 us -> 63.5 us  [body(): pl.pallas_call(functools.partial(kernel, nz, ny, nx, cap), out_shape=pltp...]
    unnamed x1, local copies, waits for them, and re-layouts: 1.87 us -> 0.8 us
where the time goes in v3:
time: 65.1 us; the launch traced here: 64.9 us
  Pallas kernels  63.5 us (98%)
  local copies, waits for them, and re-layouts  0.8 us (1%)
  between operations  0.66 us (1%)
    pallas_call x1, Pallas kernels, body(): pl.pallas_call(functools.partial(kernel, nz, ny, nx, cap), out_shape=pltp...  63.5 us

profile of v3, /device:TPU:1, one launch (start us, length us, event | category | flops | bytes accessed | tf_op | source)
XLA Modules:
  0.0 64.9 jit_solution(5004588158724351886)
XLA Ops:
  0.7 63.5 %sketch_gram.1 = f32[64,2048]{1,0:T(8,128)S(1)} custom-call(f32[2,8,2,8,8,128]{5,4,3,2,1,0:T(8,128)} %bitcast.7, f32[1,128]{1,0:T(1,128)} %bitcast.8, s32[1,4]{1,0:T(1,128)} %rows.1, s32[1,128]{1,0:T(1,128)} %bitcast.9, f32[1,1]{1,0:T(1,128)} %bitcast.5.ridge), custom_call_target="tpu_custom_call" | custom-call | tf_op jit(solution)/shard_map/sketch_gram/pallas_call | solution.py:507
  64.1 0.8 %copy.7 = f32[2048,64]{0,1:T(8,128)} copy(f32[2048,64]{0,1:T(8,128)S(1)} %bitcast.6) | data formatting | bytes 1048576

commit v4 on v3

--- a/solution.py
+++ b/solution.py
@@ -36,7 +36,7 @@
 
 SUBS = 4
 GROUP = 4
-PLAN = (((1, 3), "relay0"), ((2, 1), "relay1"), ((2, 3), "far0"), ((3, 0), "far1"), ((3, 2), "ready"))
+PLAN = (((1, 2), "relay0"), ((1, 3), "relay1"), ((2, 0), "far0"), ((2, 2), "far1"), ((2, 3), "ready"))
 
 
 def kernel(
@@ -63,16 +63,10 @@
     def up_y(d):
         return wrap(y + d, ny)
 
-    pending = []
-
-    def send(src, dst, ss, rs, to, keep=True):
-        copy = pltpu.make_async_remote_copy(
+    def send(src, dst, ss, rs, to):
+        pltpu.make_async_remote_copy(
             src_ref=src, dst_ref=dst, send_sem=ss, recv_sem=rs, device_id=to, device_id_type=MESH
-        )
-        copy.start()
-        if keep:
-            pending.append(copy)
-        return copy
+        ).start()
 
     def arrived(slot, sem):
         pltpu.make_async_copy(slot, slot, sem).wait()
@@ -116,21 +110,21 @@
 
     @pl.when(c == 0)
     def _():
-        send(sm1.at[z, 0], sm1.at[z, 0], s_sm1.at[0], r_sm1.at[0, 0], at(z, y, 1, q), keep=False)
+        send(sm1.at[z, 0], sm1.at[z, 0], s_sm1.at[0], r_sm1.at[0, 0], at(z, y, 1, q))
 
     for d in range(1, nz):
-        send(sm1.at[z, c], sm1.at[z, c], s_sm1.at[d], r_sm1.at[d, c], at(up_z(d), y, 1, q))
+        send(sm1.at[z, c], sm1.at[z, c], s_sm1.at[1], r_sm1.at[d, c], at(up_z(d), y, 1, q))
 
     def raw_z(d):
         for cc in (0, 1):
-            send(xs.at[cc, :, 0, up_z(d)], ra.at[z, c], s_raw.at[0, d, cc], r_raw.at[0, d, c], at(up_z(d), y, cc, q), keep=False)
+            send(xs.at[cc, :, 0, up_z(d)], ra.at[z, c], s_raw.at[0, 0], r_raw.at[0, d, c], at(up_z(d), y, cc, q))
 
     def raw_y(d):
         for cc in (0, 1):
-            send(xs.at[cc, up_y(d), 1], rb.at[y, c], s_raw.at[1, d, cc], r_raw.at[1, d, c], at(z, up_y(d), cc, q), keep=False)
-
-    send(xs.at[mate, :, 0, z], ra.at[z, c], s_raw.at[0, 0, 0], r_raw.at[0, 0, c], at(z, y, mate, q))
-    send(xs.at[mate, y, 1], rb.at[y, c], s_raw.at[1, 0, 0], r_raw.at[1, 0, c], at(z, y, mate, q))
+            send(xs.at[cc, up_y(d), 1], rb.at[y, c], s_raw.at[1, 0], r_raw.at[1, d, c], at(z, up_y(d), cc, q))
+
+    send(xs.at[mate, :, 0, z], ra.at[z, c], s_raw.at[0, 1], r_raw.at[0, 0, c], at(z, y, mate, q))
+    send(xs.at[mate, y, 1], rb.at[y, c], s_raw.at[1, 1], r_raw.at[1, 0, c], at(z, y, mate, q))
 
     order_z, order_y = near_first(nz), near_first(ny)
 
@@ -153,8 +147,8 @@
         sm2[y] = jnp.sum(sm1[...].reshape(2 * nz, 1, cap), axis=0)
         for d in range(1, ny):
             for cc in (0, 1):
-                send(sm2.at[y], sm2.at[y], s_sm2.at[d, cc], r_sm2.at[d], at(z, up_y(d), cc, q), keep=False)
-        send(sm2.at[y], sm2.at[y], s_sm2.at[0, 0], r_sm2.at[0], at(z, y, 0, q), keep=False)
+                send(sm2.at[y], sm2.at[y], s_sm2.at[1 + cc], r_sm2.at[d], at(z, up_y(d), cc, q))
+        send(sm2.at[y], sm2.at[y], s_sm2.at[0], r_sm2.at[0], at(z, y, 0, q))
         for d in order_y:
             raw_y(d)
 
@@ -215,13 +209,13 @@
             if k == len(steps_z) - 1:
                 pa[...] = acc_z.reshape(ny, 8, cap)
                 for d in far_first(ny):
-                    send(pa.at[up_y(d)], qa.at[y], s_red.at[0, d], r_red.at[0, d], at(z, up_y(d), c, q))
+                    send(pa.at[up_y(d)], qa.at[y], s_red.at[0], r_red.at[0], at(z, up_y(d), c, q))
         if k < len(steps_y):
             acc_y = share_of(1, steps_y[k], acc_y)
             if k == len(steps_y) - 1:
                 pb[...] = acc_y.reshape(nz, 8, cap)
                 for d in far_first(nz):
-                    send(pb.at[up_z(d)], qb.at[z], s_red.at[1, d], r_red.at[1, d], at(up_z(d), y, c, q))
+                    send(pb.at[up_z(d)], qb.at[z], s_red.at[1], r_red.at[1], at(up_z(d), y, c, q))
 
     subs = min(SUBS, nz, ny)
 
@@ -250,7 +244,7 @@
                     continue
                 step = far - d if way == 0 else n - (far - d)
                 to = at(z, up_y(step), c, q) if which == 0 else at(up_z(step), y, c, q)
-                send(view, view, s_ring.at[which, way, far - 1, k], r_ring.at[which, way, far - 1, k], to)
+                send(view, view, s_ring.at[which], r_ring.at[which, way, far - 1, k], to)
 
     def take(which, d, k):
         for way in (0, 1):
@@ -263,28 +257,28 @@
     hop = wrap(target - z + nz, nz)
 
     piece = pa[y]
+    arrived(qa.at[pl.ds(0, ny - 1)], r_red.at[0])
     for d in range(1, ny):
-        arrived(qa.at[up_y(ny - d)], r_red.at[0, d])
         piece = piece + qa[up_y(ny - d)]
     sa[y, 0] = piece
     for d in near_first(nz):
-        send(sa.at[y, 0], sa.at[y, orders[0].index(d)], s_ag.at[0, d], r_ag.at[0, d], at(up_z(d), y, c, q))
+        send(sa.at[y, 0], sa.at[y, orders[0].index(d)], s_ag.at[0], r_ag.at[0, d], at(up_z(d), y, c, q))
     piece = pb[z]
+    arrived(qb.at[pl.ds(0, nz - 1)], r_red.at[1])
     for d in range(1, nz):
-        arrived(qb.at[up_z(nz - d)], r_red.at[1, d])
         piece = piece + qb[up_z(nz - d)]
     sb[z, 0] = piece
 
     @pl.when(hop != 0)
     def _():
-        send(sb.at[z, 0], bo.at[1, z], s_op.at[hop], r_op.at[hop], at(target, y, c, q), keep=False)
+        send(sb.at[z, 0], bo.at[1, z], s_op.at[hop], r_op.at[hop], at(target, y, c, q))
 
     @pl.when(hop == 0)
     def _():
         bo[1, z] = piece
 
     for d in near_first(ny):
-        send(sb.at[z, 0], sb.at[z, orders[1].index(d)], s_ag.at[1, d], r_ag.at[1, d], at(z, up_y(d), c, q))
+        send(sb.at[z, 0], sb.at[z, orders[1].index(d)], s_ag.at[1], r_ag.at[1, d], at(z, up_y(d), c, q))
     for k in range(subs):
         for which in (0, 1):
             mine, buf = (y, sa) if which == 0 else (z, sb)
@@ -304,13 +298,13 @@
     @pl.when((c == root_c) & (away == 0))
     def _():
         for d in beside:
-            send(sa.at[y], bo.at[0], s_x.at[0, d], r_x.at[0, 0], at(z, y, c, wrap(q + d, nx)), keep=False)
-        send(sa.at[y], bo.at[0], s_sib.at[0], r_sib.at[0], at(z, y, mate, q), keep=False)
+            send(sa.at[y], bo.at[0], s_x.at[0, d], r_x.at[0, 0], at(z, y, c, wrap(q + d, nx)))
+        send(sa.at[y], bo.at[0], s_sib.at[0], r_sib.at[0], at(z, y, mate, q))
         for d in range(1, nz):
             arrived(bo.at[1, up_z(nz - d)], r_op.at[d])
         for d in beside:
-            send(bo.at[1], bo.at[1], s_x.at[1, d], r_x.at[1, 0], at(z, y, c, wrap(q + d, nx)), keep=False)
-        send(bo.at[1], bo.at[1], s_sib.at[1], r_sib.at[1], at(z, y, mate, q), keep=False)
+            send(bo.at[1], bo.at[1], s_x.at[1, d], r_x.at[1, 0], at(z, y, c, wrap(q + d, nx)))
+        send(bo.at[1], bo.at[1], s_sib.at[1], r_sib.at[1], at(z, y, mate, q))
         bo[0] = sa[y]
 
     def relay(h):
@@ -323,8 +317,8 @@
                 if nx > 2:
                     there = wrap(root_q + 2, nx)
                     view = bo.at[h, part]
-                    send(view, view, s_x.at[h, 2], r_x.at[h, d], at(z, y, c, there), keep=False)
-                send(bo.at[h], bo.at[h], s_sib.at[h], r_sib.at[h], at(z, y, mate, q), keep=False)
+                    send(view, view, s_x.at[h, 2], r_x.at[h, d], at(z, y, c, there))
+                send(bo.at[h], bo.at[h], s_sib.at[h], r_sib.at[h], at(z, y, mate, q))
 
     def relay_far(h):
         if nx > 2:
@@ -334,7 +328,7 @@
                 for d in beside:
                     view = bo.at[h, pl.ds(0 if d == 1 else mid, mid)]
                     arrived(view, r_x.at[h, d])
-                send(bo.at[h], bo.at[h], s_sib.at[h], r_sib.at[h], at(z, y, mate, q), keep=False)
+                send(bo.at[h], bo.at[h], s_sib.at[h], r_sib.at[h], at(z, y, mate, q))
 
     wide = 2 * nz * 8
     half_wide = wide // 2
@@ -442,31 +436,25 @@
         left, right = turned[:half_wide], turned[half_wide:]
         lanes = pl.ds(pl.multiple_of((c * ny + k) * wide, wide), wide)
         st[k] = jnp.where(c == 0, right, left)
-        send(st.at[k], out.at[:, lanes], s_out.at[k], r_out.at[k], at(z, y, mate, q))
+        send(st.at[k], out.at[:, lanes], s_out, r_out, at(z, y, mate, q))
         out[:, lanes] = jnp.where(c == 0, left, right)
-    for k in range(ny):
-        lanes = pl.ds(pl.multiple_of((mate * ny + k) * wide, wide), wide)
-        arrived(out.at[:, lanes], r_out.at[k])
-
-    for copy in pending:
-        copy.wait_send()
-    for d in range(1, nz):
+    for which, n, raw, red, buf in ((0, nz, ra, qa, sa), (1, ny, rb, qb, sb)):
+        sent(raw.at[pl.ds(0, n - 1)], s_raw.at[which, 0])
+        sent(raw.at[0, 0], s_raw.at[which, 1])
+        sent(red.at[pl.ds(0, red.shape[0] - 1)], s_red.at[which])
+        sent(buf.at[0, pl.ds(0, n - 1)], s_ag.at[which])
+        sent(buf.at[pl.ds(0, buf.shape[0] - 1)], s_ring.at[which])
+    sent(sm1.at[pl.ds(0, nz - 1), 0], s_sm1.at[1])
+
+    @pl.when(c == 0)
+    def _():
+        sent(sm1.at[0, 0], s_sm1.at[0])
+
+    @pl.when(c == 1)
+    def _():
         for cc in (0, 1):
-            sent(ra.at[0, 0], s_raw.at[0, d, cc])
-    for d in range(1, ny):
-        for cc in (0, 1):
-            sent(rb.at[0, 0], s_raw.at[1, d, cc])
-
-    @pl.when(c == 0)
-    def _():
-        sent(sm1.at[0, 0], s_sm1.at[0])
-
-    @pl.when(c == 1)
-    def _():
-        for d in range(1, ny):
-            for cc in (0, 1):
-                sent(sm2.at[0], s_sm2.at[d, cc])
-        sent(sm2.at[0], s_sm2.at[0, 0])
+            sent(sm2.at[pl.ds(0, ny - 1)], s_sm2.at[1 + cc])
+        sent(sm2.at[0], s_sm2.at[0])
 
     @pl.when(hop != 0)
     def _():
@@ -489,6 +477,9 @@
     def _():
         for h in (0, 1):
             sent(bo.at[h], s_sib.at[h])
+
+    sent(st, s_out)
+    arrived(out.at[:, pl.ds(pl.multiple_of(mate * (ny * wide), wide), ny * wide)], r_out)
 
 
 def body(hidden_panel, row_signs, sample_rows, sample_counts, ridge_weight):
@@ -528,15 +519,15 @@
             pltpu.VMEM((ny, 2, nz, 8, 2 * half_wide), f32),
             pltpu.VMEM((ny, half_wide, 2 * half_wide), f32),
             dma(()),
+            dma((2, 2)),
             dma((2, m, 2)),
-            dma((2, m, 2)),
-            dma((nz,)),
+            dma((2,)),
             dma((nz, 2)),
-            dma((ny, 2)),
+            dma((3,)),
             dma((ny,)),
-            dma((2, m)),
-            dma((2, m)),
-            dma((2, m)),
+            dma((2,)),
+            dma((2,)),
+            dma((2,)),
             dma((2, m)),
             dma((nz,)),
             dma((nz,)),
@@ -544,10 +535,10 @@
             dma((2, nx)),
             dma((2,)),
             dma((2,)),
+            dma((2,)),
             dma((2, 2, m // 2, m)),
-            dma((2, 2, m // 2, m)),
-            dma((ny,)),
-            dma((ny,)),
+            dma(()),
+            dma(()),
         ],
         compiler_params=pltpu.CompilerParams(collective_id=0, has_side_effects=True),
         name="sketch_gram",

time: 65.1 us -> 62.6 us (0.962)
  Pallas kernels: 63.5 us -> 61 us
    pallas_call x1, Pallas kernels: 63.5 us -> 61 us  [body(): pl.pallas_call(functools.partial(kernel, nz, ny, nx, cap), out_shape=pltp...]
where the time goes in v4:
time: 62.6 us; the launch traced here: 62.4 us
  Pallas kernels  61 us (97%)
  local copies, waits for them, and re-layouts  0.8 us (1%)
  between operations  0.66 us (1%)
    pallas_call x1, Pallas kernels, body(): pl.pallas_call(functools.partial(kernel, nz, ny, nx, cap), out_shape=pltp...  61 us

profile of v4, /device:TPU:1, one launch (start us, length us, event | category | flops | bytes accessed | tf_op | source)
XLA Modules:
  0.0 62.4 jit_solution(13210619640908258512)
XLA Ops:
  0.7 61.0 %sketch_gram.1 = f32[64,2048]{1,0:T(8,128)S(1)} custom-call(f32[2,8,2,8,8,128]{5,4,3,2,1,0:T(8,128)} %bitcast.7, f32[1,128]{1,0:T(1,128)} %bitcast.8, s32[1,4]{1,0:T(1,128)} %rows.1, s32[1,128]{1,0:T(1,128)} %bitcast.9, f32[1,1]{1,0:T(1,128)} %bitcast.5.ridge), custom_call_target="tpu_custom_call" | custom-call | tf_op jit(solution)/shard_map/sketch_gram/pallas_call | solution.py:498
  61.6 0.8 %copy.7 = f32[2048,64]{0,1:T(8,128)} copy(f32[2048,64]{0,1:T(8,128)S(1)} %bitcast.6) | data formatting | bytes 1048576

commit v5 on v4

--- a/solution.py
+++ b/solution.py
@@ -110,21 +110,21 @@
 
     @pl.when(c == 0)
     def _():
-        send(sm1.at[z, 0], sm1.at[z, 0], s_sm1.at[0], r_sm1.at[0, 0], at(z, y, 1, q))
+        send(sm1.at[z, 0], sm1.at[z, 0], s_sm1.at[0], r_sm1.at[0], at(z, y, 1, q))
 
     for d in range(1, nz):
-        send(sm1.at[z, c], sm1.at[z, c], s_sm1.at[1], r_sm1.at[d, c], at(up_z(d), y, 1, q))
+        send(sm1.at[z, c], sm1.at[z, c], s_sm1.at[1], r_sm1.at[1], at(up_z(d), y, 1, q))
 
     def raw_z(d):
         for cc in (0, 1):
-            send(xs.at[cc, :, 0, up_z(d)], ra.at[z, c], s_raw.at[0, 0], r_raw.at[0, d, c], at(up_z(d), y, cc, q))
+            send(xs.at[cc, :, 0, up_z(d)], ra.at[z, c], s_raw.at[0, 0], r_raw.at[0, d], at(up_z(d), y, cc, q))
 
     def raw_y(d):
         for cc in (0, 1):
-            send(xs.at[cc, up_y(d), 1], rb.at[y, c], s_raw.at[1, 0], r_raw.at[1, d, c], at(z, up_y(d), cc, q))
-
-    send(xs.at[mate, :, 0, z], ra.at[z, c], s_raw.at[0, 1], r_raw.at[0, 0, c], at(z, y, mate, q))
-    send(xs.at[mate, y, 1], rb.at[y, c], s_raw.at[1, 1], r_raw.at[1, 0, c], at(z, y, mate, q))
+            send(xs.at[cc, up_y(d), 1], rb.at[y, c], s_raw.at[1, 0], r_raw.at[1, d], at(z, up_y(d), cc, q))
+
+    send(xs.at[mate, :, 0, z], ra.at[z, c], s_raw.at[0, 1], r_raw.at[0, 0], at(z, y, mate, q))
+    send(xs.at[mate, y, 1], rb.at[y, c], s_raw.at[1, 1], r_raw.at[1, 0], at(z, y, mate, q))
 
     order_z, order_y = near_first(nz), near_first(ny)
 
@@ -140,14 +140,12 @@
     def _():
         for d in order_z:
             raw_z(d)
-        arrived(sm1.at[z, 0], r_sm1.at[0, 0])
-        for d in range(1, nz):
-            for cc in (0, 1):
-                arrived(sm1.at[up_z(nz - d), cc], r_sm1.at[d, cc])
+        arrived(sm1.at[z, 0], r_sm1.at[0])
+        arrived(sm1.at[pl.ds(0, nz - 1)], r_sm1.at[1])
         sm2[y] = jnp.sum(sm1[...].reshape(2 * nz, 1, cap), axis=0)
         for d in range(1, ny):
             for cc in (0, 1):
-                send(sm2.at[y], sm2.at[y], s_sm2.at[1 + cc], r_sm2.at[d], at(z, up_y(d), cc, q))
+                send(sm2.at[y], sm2.at[y], s_sm2.at[1 + cc], r_sm2.at[1], at(z, up_y(d), cc, q))
         send(sm2.at[y], sm2.at[y], s_sm2.at[0], r_sm2.at[0], at(z, y, 0, q))
         for d in order_y:
             raw_y(d)
@@ -156,8 +154,7 @@
     def _():
         arrived(sm2.at[y], r_sm2.at[0])
 
-    for d in range(1, ny):
-        arrived(sm2.at[up_y(ny - d)], r_sm2.at[d])
+    arrived(sm2.at[pl.ds(0, ny - 1)], r_sm2.at[1])
     local_row = jnp.sum(sm2[...], axis=0)
 
     token = lax.broadcasted_iota(jnp.int32, (length, cap), 0)
@@ -196,7 +193,10 @@
                     parts.append((flat(held), block_of(z, y, c)))
                     continue
                 source = mate if d == 0 else cc
-                arrived(buf.at[far, source], r_raw.at[which, d, source])
+                if cc == 0:
+                    arrived(buf.at[far], r_raw.at[which, d])
+                elif d == 0:
+                    arrived(buf.at[far, source], r_raw.at[which, 0])
                 block_at = block_of(far, y, source) if which == 0 else block_of(z, far, source)
                 parts.append((flat(buf[far, source]), block_at))
         return share(parts, acc)
@@ -262,7 +262,7 @@
         piece = piece + qa[up_y(ny - d)]
     sa[y, 0] = piece
     for d in near_first(nz):
-        send(sa.at[y, 0], sa.at[y, orders[0].index(d)], s_ag.at[0], r_ag.at[0, d], at(up_z(d), y, c, q))
+        send(sa.at[y, 0], sa.at[y, orders[0].index(d)], s_ag.at[0], r_ag.at[0, orders[0].index(d) * subs // nz], at(up_z(d), y, c, q))
     piece = pb[z]
     arrived(qb.at[pl.ds(0, nz - 1)], r_red.at[1])
     for d in range(1, nz):
@@ -271,22 +271,21 @@
 
     @pl.when(hop != 0)
     def _():
-        send(sb.at[z, 0], bo.at[1, z], s_op.at[hop], r_op.at[hop], at(target, y, c, q))
+        send(sb.at[z, 0], bo.at[1, z], s_op, r_op, at(target, y, c, q))
 
     @pl.when(hop == 0)
     def _():
         bo[1, z] = piece
 
     for d in near_first(ny):
-        send(sb.at[z, 0], sb.at[z, orders[1].index(d)], s_ag.at[1], r_ag.at[1, d], at(z, up_y(d), c, q))
+        send(sb.at[z, 0], sb.at[z, orders[1].index(d)], s_ag.at[1], r_ag.at[1, orders[1].index(d) * subs // ny], at(z, up_y(d), c, q))
     for k in range(subs):
         for which in (0, 1):
             mine, buf = (y, sa) if which == 0 else (z, sb)
             size = buf.shape[1] // subs
-            for place_of in range(k * size, (k + 1) * size):
-                e = orders[which][place_of]
-                if e:
-                    arrived(buf.at[mine, place_of], r_ag.at[which, e])
+            begin = max(k * size, 1)
+            if begin < (k + 1) * size:
+                arrived(buf.at[mine, pl.ds(begin, (k + 1) * size - begin)], r_ag.at[which, k])
             pass_on(which, 0, k)
 
     root_c = wrap(z, 2)
@@ -300,8 +299,7 @@
         for d in beside:
             send(sa.at[y], bo.at[0], s_x.at[0, d], r_x.at[0, 0], at(z, y, c, wrap(q + d, nx)))
         send(sa.at[y], bo.at[0], s_sib.at[0], r_sib.at[0], at(z, y, mate, q))
-        for d in range(1, nz):
-            arrived(bo.at[1, up_z(nz - d)], r_op.at[d])
+        arrived(bo.at[1, pl.ds(0, nz - 1)], r_op)
         for d in beside:
             send(bo.at[1], bo.at[1], s_x.at[1, d], r_x.at[1, 0], at(z, y, c, wrap(q + d, nx)))
         send(bo.at[1], bo.at[1], s_sib.at[1], r_sib.at[1], at(z, y, mate, q))
@@ -458,7 +456,7 @@
 
     @pl.when(hop != 0)
     def _():
-        sent(sb.at[z, 0], s_op.at[hop])
+        sent(sb.at[z, 0], s_op)
 
     @pl.when((c == root_c) & (away == 0))
     def _():
@@ -520,17 +518,17 @@
             pltpu.VMEM((ny, half_wide, 2 * half_wide), f32),
             dma(()),
             dma((2, 2)),
-            dma((2, m, 2)),
-            dma((2,)),
-            dma((nz, 2)),
+            dma((2, m)),
+            dma((2,)),
+            dma((2,)),
             dma((3,)),
-            dma((ny,)),
+            dma((2,)),
             dma((2,)),
             dma((2,)),
             dma((2,)),
             dma((2, m)),
-            dma((nz,)),
-            dma((nz,)),
+            dma(()),
+            dma(()),
             dma((2, nx)),
             dma((2, nx)),
             dma((2,)),

time: 62.6 us -> 62.2 us (level)
  no operation moved by 1% of the time
where the time goes in v5:
time: 62.2 us; the launch traced here: 62.1 us
  Pallas kernels  60.6 us (97%)
  local copies, waits for them, and re-layouts  0.8 us (1%)
  between operations  0.66 us (1%)
    pallas_call x1, Pallas kernels, body(): pl.pallas_call(functools.partial(kernel, nz, ny, nx, cap), out_shape=pltp...  60.6 us

profile of v5, /device:TPU:1, one launch (start us, length us, event | category | flops | bytes accessed | tf_op | source)
XLA Modules:
  0.0 62.1 jit_solution(4264825541498727225)
XLA Ops:
  0.7 60.6 %sketch_gram.1 = f32[64,2048]{1,0:T(8,128)S(1)} custom-call(f32[2,8,2,8,8,128]{5,4,3,2,1,0:T(8,128)} %bitcast.7, f32[1,128]{1,0:T(1,128)} %bitcast.8, s32[1,4]{1,0:T(1,128)} %rows.1, s32[1,128]{1,0:T(1,128)} %bitcast.9, f32[1,1]{1,0:T(1,128)} %bitcast.5.ridge), custom_call_target="tpu_custom_call" | custom-call | tf_op jit(solution)/shard_map/sketch_gram/pallas_call | solution.py:496
  61.3 0.8 %copy.7 = f32[2048,64]{0,1:T(8,128)} copy(f32[2048,64]{0,1:T(8,128)S(1)} %bitcast.6) | data formatting | bytes 1048576

commit v6 on v5

--- a/solution.py
+++ b/solution.py
@@ -486,67 +486,73 @@
     ny = lax.axis_size("rows") // (2 * nz)
     width, length = hidden_panel.shape
     shards = sample_counts.shape[0]
-    cap = -(-shards * sample_rows.shape[1] // 128) * 128
+    full = -(-shards * sample_rows.shape[1] // 128) * 128
     half_wide = 8 * nz
     dma, f32, i32, bf16 = pltpu.SemaphoreType.DMA, jnp.float32, jnp.int32, jnp.bfloat16
     m = max(nz, ny)
     vmem = pl.BlockSpec(memory_space=pltpu.VMEM)
     smem = pl.BlockSpec(memory_space=pltpu.SMEM)
     hbm = pl.BlockSpec(memory_space=pl.ANY)
-    result = pl.pallas_call(
-        functools.partial(kernel, nz, ny, nx, cap),
-        out_shape=pltpu.VMEM((half_wide, width), f32),
-        in_specs=[hbm, vmem, smem, vmem, smem],
-        out_specs=vmem,
-        scratch_shapes=[
-            pltpu.VMEM((2, ny, 2, nz, 8, length), f32),
-            pltpu.VMEM((nz, 2, ny, 8, length), f32),
-            pltpu.VMEM((ny, 2, nz, 8, length), f32),
-            pltpu.VMEM((nz, 2, 1, cap), i32),
-            pltpu.VMEM((ny, 1, cap), i32),
-            pltpu.VMEM((ny, 8, cap), f32),
-            pltpu.VMEM((nz, 8, cap), f32),
-            pltpu.VMEM((ny, 8, cap), f32),
-            pltpu.VMEM((nz, 8, cap), f32),
-            pltpu.VMEM((ny, nz, 8, cap), f32),
-            pltpu.VMEM((nz, ny, 8, cap), f32),
-            pltpu.VMEM((2, nz, 8, cap), f32),
-            pltpu.VMEM((nz, 8, cap), f32),
-            pltpu.VMEM((cap, 4 * half_wide), bf16),
-            pltpu.VMEM((2 * length, cap), bf16),
-            pltpu.VMEM((ny, 2, nz, 8, 2 * half_wide), f32),
-            pltpu.VMEM((ny, half_wide, 2 * half_wide), f32),
-            dma(()),
-            dma((2, 2)),
-            dma((2, m)),
-            dma((2,)),
-            dma((2,)),
-            dma((3,)),
-            dma((2,)),
-            dma((2,)),
-            dma((2,)),
-            dma((2,)),
-            dma((2, m)),
-            dma(()),
-            dma(()),
-            dma((2, nx)),
-            dma((2, nx)),
-            dma((2,)),
-            dma((2,)),
-            dma((2,)),
-            dma((2, 2, m // 2, m)),
-            dma(()),
-            dma(()),
-        ],
-        compiler_params=pltpu.CompilerParams(collective_id=0, has_side_effects=True),
-        name="sketch_gram",
-    )(
-        hidden_panel.reshape(2, ny, 2, nz, 8, length),
-        row_signs.reshape(1, length),
-        sample_rows,
-        sample_counts.reshape(1, shards),
-        ridge_weight.reshape(1, 1),
-    )
+    def run(cap, number):
+        return pl.pallas_call(
+            functools.partial(kernel, nz, ny, nx, cap),
+            out_shape=pltpu.VMEM((half_wide, width), f32),
+            in_specs=[hbm, vmem, smem, vmem, smem],
+            out_specs=vmem,
+            scratch_shapes=[
+                pltpu.VMEM((2, ny, 2, nz, 8, length), f32),
+                pltpu.VMEM((nz, 2, ny, 8, length), f32),
+                pltpu.VMEM((ny, 2, nz, 8, length), f32),
+                pltpu.VMEM((nz, 2, 1, cap), i32),
+                pltpu.VMEM((ny, 1, cap), i32),
+                pltpu.VMEM((ny, 8, cap), f32),
+                pltpu.VMEM((nz, 8, cap), f32),
+                pltpu.VMEM((ny, 8, cap), f32),
+                pltpu.VMEM((nz, 8, cap), f32),
+                pltpu.VMEM((ny, nz, 8, cap), f32),
+                pltpu.VMEM((nz, ny, 8, cap), f32),
+                pltpu.VMEM((2, nz, 8, cap), f32),
+                pltpu.VMEM((nz, 8, cap), f32),
+                pltpu.VMEM((cap, 4 * half_wide), bf16),
+                pltpu.VMEM((2 * length, cap), bf16),
+                pltpu.VMEM((ny, 2, nz, 8, 2 * half_wide), f32),
+                pltpu.VMEM((ny, half_wide, 2 * half_wide), f32),
+                dma(()),
+                dma((2, 2)),
+                dma((2, m)),
+                dma((2,)),
+                dma((2,)),
+                dma((3,)),
+                dma((2,)),
+                dma((2,)),
+                dma((2,)),
+                dma((2,)),
+                dma((2, m)),
+                dma(()),
+                dma(()),
+                dma((2, nx)),
+                dma((2, nx)),
+                dma((2,)),
+                dma((2,)),
+                dma((2,)),
+                dma((2, 2, m // 2, m)),
+                dma(()),
+                dma(()),
+            ],
+            compiler_params=pltpu.CompilerParams(collective_id=number, has_side_effects=True),
+            name="sketch_gram",
+        )(
+            hidden_panel.reshape(2, ny, 2, nz, 8, length),
+            row_signs.reshape(1, length),
+            sample_rows,
+            sample_counts.reshape(1, shards),
+            ridge_weight.reshape(1, 1),
+        )
+
+    small = full * 3 // 512 * 128
+    if small == 0:
+        return run(full, 0).T
+    result = lax.cond(jnp.sum(sample_counts) <= small, lambda: run(small, 1), lambda: run(full, 0))
     return result.T
 
 

time: 62.2 us -> 61.2 us (0.984)
  Pallas kernels: 60.6 us -> 57.4 us
  other arithmetic: 0 us -> 1.29 us
  local copies, waits for them, and re-layouts: 0.8 us -> 1.46 us
    pallas_call x1, Pallas kernels: 60.6 us -> 57.4 us  [run(): pl.pallas_call(functools.partial(kernel, nz, ny, nx, cap), out_shape=pltp...]
    reduce_sum x0 -> x1, other arithmetic: none -> 1.29 us  [body(): jnp.sum(sample_counts) <= small]
    unnamed x1 -> x7, local copies, waits for them, and re-layouts: 0.8 us -> 1.46 us
where the time goes in v6:
time: 61.2 us; the launch traced here: 60.9 us
  Pallas kernels  57.4 us (94%)
  local copies, waits for them, and re-layouts  1.46 us (2%)
  other arithmetic  1.29 us (2%)
  between operations  0.69 us (1%)
    pallas_call x1, Pallas kernels, run(): pl.pallas_call(functools.partial(kernel, nz, ny, nx, cap), out_shape=pltp...  57.4 us
    unnamed x7, local copies, waits for them, and re-layouts  1.46 us
    reduce_sum x1, other arithmetic, body(): jnp.sum(sample_counts) <= small  1.29 us

profile of v6, /device:TPU:1, one launch (start us, length us, event | category | flops | bytes accessed | tf_op | source)
XLA Modules:
  0.0 60.9 jit_solution(13618959924614835326)
XLA Ops:
  0.0 1.3 %reduce_sum.9 = s32[]{:T(128)} reduce(s32[128]{0:T(128)} %param.10, s32[]{:T(128)} %constant.0.clone.1), dimensions={0}, to_apply=%region_0.0 | reduce | flops 127 | bytes 520 | tf_op jit(solution)/shard_map/reduce_sum | solution.py:555
  1.9 0.0 copy-start
  2.0 0.0 copy-start.1
  2.0 0.0 copy-start.2
  2.0 0.6 %copy-done = s32[128]{0:T(128)S(1)} copy-done((s32[128]{0:T(128)S(1)}, s32[128]{0:T(128)}, u32[]{:S(2)}) %copy-start) | copy-done | bytes 536
  2.6 0.0 copy-done.1
  2.6 0.0 copy-done.2
  2.6 57.4 %conditional.1 = (f32[64,2048]{1,0:T(8,128)S(1)}) conditional(s32[]{:T(128)} %convert_element_type.3, (f32[2048,128]{1,0:T(8,128)}, f32[128]{0:T(128)S(1)}, s32[128]{0:T(128)S(1)}, f32[]{:T(128)}, s32[1,4]{1,0:T(1,128)S(1)}) %tuple.18, (f32[2048,128]{1,0:T(8,128)}, f32[128]{0:T(128)S(1)}, s32[128]{0:T(128)S(1)}, f32[]{:T(128)}, ...), branch_computations={%region_1.0_spmd, %region_2.0_spmd} | conditional | bytes 8 | solution.py:555
  2.6 57.4 %sketch_gram.3 = f32[64,2048]{1,0:T(8,128)S(1)} custom-call(f32[2,8,2,8,8,128]{5,4,3,2,1,0:T(8,128)} %bitcast.11, f32[1,128]{1,0:T(1,128)S(1)} %bitcast.15, s32[1,4]{1,0:T(1,128)S(1)} %get-tuple-element.35.rows, s32[1,128]{1,0:T(1,128)S(1)} %bitcast.13, f32[1,1]{1,0:T(1,128)} %bitcast.7.ridge), custom_call_target="tpu_custom_call" | custom-call | tf_op jit(solution)/shard_map/cond/branch_1_fun/sketch_gram/pallas_call | solution.py:497
  60.1 0.8 %copy.9 = f32[2048,64]{0,1:T(8,128)} copy(f32[2048,64]{0,1:T(8,128)S(1)} %bitcast.9) | data formatting | bytes 1048576
Async XLA Ops:
  1.9 0.7 %copy-start = (s32[128]{0:T(128)S(1)}, s32[128]{0:T(128)}, u32[]{:S(2)}) copy-start(s32[128]{0:T(128)} %param.10) | copy-start | bytes 1540
  2.0 0.7 %copy-start.1 = (f32[128]{0:T(128)S(1)}, f32[128]{0:T(128)}, u32[]{:S(2)}) copy-start(f32[128]{0:T(128)} %param.8) | copy-start | bytes 1540
  2.0 0.7 %copy-start.2 = (s32[1,4]{1,0:T(1,128)S(1)}, s32[1,4]{1,0:T(1,128)}, u32[]{:S(2)}) copy-start(s32[1,4]{1,0:T(1,128)} %param.9) | copy-start | bytes 52

commit v7 on v6

--- a/solution.py
+++ b/solution.py
@@ -412,7 +412,7 @@
     done = 0
     for d in range(1, top + 1):
         for k in range(subs):
-            for which in (0, 1):
+            for which in (1, 0):
                 if d <= extent[which] // 2:
                     take(which, d, k)
             for now, act in PLAN:

time: 61.2 us -> 61.4 us (level)
  no operation moved by 1% of the time
where the time goes in v7:
time: 61.4 us; the launch traced here: 61.2 us
  Pallas kernels  57.8 us (94%)
  local copies, waits for them, and re-layouts  1.46 us (2%)
  other arithmetic  1.29 us (2%)
  between operations  0.69 us (1%)
    pallas_call x1, Pallas kernels, run(): pl.pallas_call(functools.partial(kernel, nz, ny, nx, cap), out_shape=pltp...  57.8 us
    unnamed x7, local copies, waits for them, and re-layouts  1.46 us
    reduce_sum x1, other arithmetic, body(): jnp.sum(sample_counts) <= small  1.29 us

profile of v7, /device:TPU:1, one launch (start us, length us, event | category | flops | bytes accessed | tf_op | source)
XLA Modules:
  0.0 61.2 jit_solution(12266662416120154660)
XLA Ops:
  0.0 1.3 %reduce_sum.9 = s32[]{:T(128)} reduce(s32[128]{0:T(128)} %param.10, s32[]{:T(128)} %constant.0.clone.1), dimensions={0}, to_apply=%region_0.0 | reduce | flops 127 | bytes 520 | tf_op jit(solution)/shard_map/reduce_sum | solution.py:555
  1.9 0.0 copy-start
  2.0 0.0 copy-start.1
  2.0 0.0 copy-start.2
  2.0 0.6 %copy-done = s32[128]{0:T(128)S(1)} copy-done((s32[128]{0:T(128)S(1)}, s32[128]{0:T(128)}, u32[]{:S(2)}) %copy-start) | copy-done | bytes 536
  2.6 0.0 copy-done.1
  2.6 0.0 copy-done.2
  2.6 57.8 %conditional.1 = (f32[64,2048]{1,0:T(8,128)S(1)}) conditional(s32[]{:T(128)} %convert_element_type.3, (f32[2048,128]{1,0:T(8,128)}, f32[128]{0:T(128)S(1)}, s32[128]{0:T(128)S(1)}, f32[]{:T(128)}, s32[1,4]{1,0:T(1,128)S(1)}) %tuple.18, (f32[2048,128]{1,0:T(8,128)}, f32[128]{0:T(128)S(1)}, s32[128]{0:T(128)S(1)}, f32[]{:T(128)}, ...), branch_computations={%region_1.0_spmd, %region_2.0_spmd} | conditional | bytes 8 | solution.py:555
  2.6 57.8 %sketch_gram.3 = f32[64,2048]{1,0:T(8,128)S(1)} custom-call(f32[2,8,2,8,8,128]{5,4,3,2,1,0:T(8,128)} %bitcast.11, f32[1,128]{1,0:T(1,128)S(1)} %bitcast.15, s32[1,4]{1,0:T(1,128)S(1)} %get-tuple-element.35.rows, s32[1,128]{1,0:T(1,128)S(1)} %bitcast.13, f32[1,1]{1,0:T(1,128)} %bitcast.7.ridge), custom_call_target="tpu_custom_call" | custom-call | tf_op jit(solution)/shard_map/cond/branch_1_fun/sketch_gram/pallas_call | solution.py:497
  60.4 0.8 %copy.9 = f32[2048,64]{0,1:T(8,128)} copy(f32[2048,64]{0,1:T(8,128)S(1)} %bitcast.9) | data formatting | bytes 1048576
Async XLA Ops:
  1.9 0.7 %copy-start = (s32[128]{0:T(128)S(1)}, s32[128]{0:T(128)}, u32[]{:S(2)}) copy-start(s32[128]{0:T(128)} %param.10) | copy-start | bytes 1540
  2.0 0.7 %copy-start.1 = (f32[128]{0:T(128)S(1)}, f32[128]{0:T(128)}, u32[]{:S(2)}) copy-start(f32[128]{0:T(128)} %param.8) | copy-start | bytes 1540
  2.0 0.7 %copy-start.2 = (s32[1,4]{1,0:T(1,128)S(1)}, s32[1,4]{1,0:T(1,128)}, u32[]{:S(2)}) copy-start(s32[1,4]{1,0:T(1,128)} %param.9) | copy-start | bytes 52
